TPU v7x, 512 devices: a whole 4x8x8 slice. The times are simulated.
512 devices in a mesh: tm: 16 (over x_lo, z), tile: 32 (over y, x_hi, core).
Axes of the slice: x: 4 (x_hi: 2, x_lo: 2; x = x_hi * 2 + x_lo), y: 8, z: 8, core: 2. Of those that a mesh axis runs over, the one named last changes fastest.
Arguments:
- anomalies: bfloat16 [512, 512, 1440], P('tm', 'tile'), may hold values from -48 to 48
- initial: bfloat16 [16, 512, 1440], P(None, 'tile'), may hold values from -6 to 6
- diffusivity: float32 [512, 1440], P('tile'), may hold values from 0.1 to 1
- land_mask: int32 [512, 1440], P('tile'), may hold values 0 or 1
- threshold: float32 [16], replicated, may hold values from 2 to 8
Outputs:
- loadings: float32 [16, 512, 1440], P(None, 'tile')
- scores: float32 [512, 16], P('tm')
All inputs are finite; a program needn't handle non-finite values. No bound on the sum of `land_mask` on one device may be relied on, other than what follows from the above.
Results may differ from a plain program's by a relative error of at most 0.0013.
The roundings to bfloat16 on the way count: a program that leaves them out, or rounds other values in their place, can miss the bound.
Values sent between devices are 32-bit elements; how exact they have to be, the bound alone decides.
A program may use at most 64 MiB of HBM per device.

v0:
```python
import math

import jax
import jax.numpy as jnp
from jax import lax
from jax.sharding import PartitionSpec as P

ITERS = 2


EPS = 1e-06
SHRINK = 0.2


def extended(block, sides, width):
    for axis, dim in sides:
        count = lax.axis_size(axis)
        forward = [(i, i + 1) for i in range(count - 1)]
        backward = [(target, source) for source, target in forward]
        low = lax.ppermute(
            lax.slice_in_dim(block, block.shape[dim] - width, None, axis=dim), axis, forward
        )
        high = lax.ppermute(lax.slice_in_dim(block, 0, width, axis=dim), axis, backward)
        block = jnp.concatenate([low, block, high], axis=dim)
    return block


def copy_for_each(shard, axis):
    copies = jnp.broadcast_to(shard, (lax.axis_size(axis), *shard.shape))
    return lax.all_to_all(copies, axis, split_axis=0, concat_axis=0, tiled=True)


def of_everyone(shard, axis):
    everything = copy_for_each(shard, axis)
    return jnp.sum(everything, axis=0)


def together(arrays, axis):
    ends = [0]
    for a in arrays:
        ends.append(ends[-1] + a.size)
    running = of_everyone(jnp.concatenate([a.ravel() for a in arrays]), axis)
    return tuple((running[b:e].reshape(a.shape) for a, b, e in zip(arrays, ends, ends[1:])))


def cut_along(shard, dim, count):
    before, after = (shard.shape[:dim], shard.shape[dim + 1 :])
    return jnp.moveaxis(shard.reshape(*before, count, -1, *after), dim, 0)


def sent_and_summed(shard, axis, dim):
    tiles = cut_along(shard, dim, lax.axis_size(axis))
    arrived = lax.all_to_all(tiles, axis, split_axis=0, concat_axis=0, tiled=True)
    return arrived.sum(axis=0)


def laid_out(tiles, dim):
    dims = list(tiles.shape[1:])
    dims[dim] *= tiles.shape[0]
    return jnp.moveaxis(tiles, 0, dim).reshape(dims)


def collect(shard, axis, dim):
    return laid_out(copy_for_each(shard, axis), dim)


def stencil_weights(diffusivity, land_mask, row_start, lat_total):
    row_index = (row_start + jnp.arange(diffusivity.shape[0], dtype=jnp.int32)).astype(jnp.float32)
    centre = jnp.sin(jnp.pi * (row_index + 0.5) / lat_total)[:, None]
    north_face = jnp.sin(jnp.pi * (row_index + 1.0) / lat_total)[:, None]
    south_face = jnp.sin(jnp.pi * row_index / lat_total)[:, None]
    diffuse = diffusivity * (1.0 + land_mask.astype(jnp.float32)) * 0.5
    return (diffuse, SHRINK * north_face / centre, SHRINK * south_face / centre)


def relax(fields, weights):
    diffuse, north_coef, south_coef = weights
    padded = extended(fields, (("tile", 1),), 1)
    eastward = jnp.roll(fields, -1, 2)
    westward = jnp.roll(fields, 1, 2)
    upper_row = padded[:, 2:, :]
    lower_row = padded[:, :-2, :]
    change = (
        SHRINK * (eastward + westward - 2.0 * fields)
        + north_coef * (upper_row - fields)
        + south_coef * (lower_row - fields)
    )
    return fields + diffuse * change


def smooth(fields, weights):
    for pass_index in range(2):
        fields = relax(fields, weights)
    return fields


def prune(values, threshold):
    return jnp.sign(values) * jnp.maximum(jnp.abs(values) - threshold[:, None, None], 0.0)


def squares(current):
    return jnp.sum(current * current, axis=(1, 2))


def local(anomalies, initial, diffusivity, land_mask, threshold):
    time_rows = anomalies.shape[0]
    lat_rows = anomalies.shape[1]
    lon_cells = anomalies.shape[2]
    mode_count = initial.shape[0]
    cell_total = lat_rows * lon_cells * lax.axis_size("tile")
    weights = stencil_weights(
        diffusivity, land_mask, lax.axis_index("tile") * lat_rows, lat_rows * lax.axis_size("tile")
    )
    mode_share = mode_count // lax.axis_size("tm")
    share_threshold = lax.dynamic_slice_in_dim(
        threshold, lax.axis_index("tm") * mode_share, mode_share, 0
    )
    flattened = anomalies.reshape(time_rows, lat_rows * lon_cells)
    current = initial.astype(jnp.float32)
    rounded = initial
    factor = jnp.ones((mode_count,), jnp.float32)
    scores = jnp.zeros((time_rows, mode_count), jnp.float32)
    for step_index in range(ITERS):
        partial_value = lax.dot_general(
            flattened,
            rounded.reshape(mode_count, lat_rows * lon_cells),
            (((1,), (1,)), ((), ())),
            preferred_element_type=jnp.float32,
        )
        partial_value, totals = together((partial_value, squares(current)), "tile")
        factor = lax.rsqrt(totals / cell_total + EPS)
        scores = partial_value * factor / math.sqrt(cell_total)
        local_sum = lax.dot_general(
            scores.astype(jnp.bfloat16),
            flattened,
            (((0,), (0,)), ((), ())),
            preferred_element_type=jnp.float32,
        )
        local_sum = local_sum.reshape(mode_count, lat_rows, lon_cells)
        portion = sent_and_summed(local_sum, "tm", 0)
        pruned = prune(smooth(portion, weights), share_threshold)
        current = collect(pruned, "tm", 0)
        rounded = current.astype(jnp.bfloat16)
    totals = of_everyone(squares(current), "tile")
    factor = lax.rsqrt(totals / cell_total + EPS)
    return (current * factor[:, None, None], scores)


def solution(mesh):
    return jax.shard_map(
        local,
        mesh=mesh,
        in_specs=(
            P("tm", "tile", None),
            P(None, "tile", None),
            P("tile", None),
            P("tile", None),
            P(),
        ),
        out_specs=(P(None, "tile", None), P("tm", None)),
        check_vma=False,
    )
```

profile of v0, /device:TPU:1, one launch (start us, length us, event | category | flops | bytes accessed | tf_op | source)
XLA Modules:
  0.0 287.4 jit_solution(4416364108694222784)
XLA Ops:
  2.0 4.3 %fusion.7 = f32[32,16]{1,0:T(8,128)S(1)} fusion(bf16[32,16,1440]{2,1,0:T(8,128)(2,1)} %param.5, bf16[16,16,1440]{2,1,0:T(8,128)(2,1)} %param.6), kind=kOutput, calls=%fused_computation.14 | convolution fusion | flops 23592960 | bytes 2213888 | tf_op jit(solution)/shard_map/dot_general | solution.py:124
  7.1 11.2 %all-to-all-start = ((f32[32,1,528]{2,1,0:T(1,128)}), f32[32,1,528]{2,1,0:T(1,128)S(1)}, u32[]{:S(2)}, u32[]{:S(2)}) async-start(f32[32,1,528]{2,1,0:T(1,128)} %broadcast_in_dim.12), calls=%async_computation | async-start | bytes 163840 | tf_op jit(solution)/shard_map/all_to_all | solution.py:30
  18.3 2.4 reshape.357
  20.7 2.5 reshape.358
  23.2 5.1 %all-to-all-done = f32[32,1,528]{2,1,0:T(1,128)S(1)} async-done(((f32[32,1,528]{2,1,0:T(1,128)}), f32[32,1,528]{2,1,0:T(1,128)S(1)}, u32[]{:S(2)}, u32[]{:S(2)}) %all-to-all-start) | async-done | bytes 67616 | tf_op jit(solution)/shard_map/all_to_all | solution.py:30
  28.5 1.8 convolution_bitcast_fusion.1
  30.3 2.1 copy.52
  32.3 10.3 %all-to-all-start.1 = ((f32[16,1,16,1440]{3,2,1,0:T(8,128)}), f32[16,1,16,1440]{3,2,1,0:T(8,128)S(1)}, u32[]{:S(2)}, u32[]{:S(2)}) async-start(f32[16,1,16,1440]{3,2,1,0:T(8,128)} %copy.52), calls=%async_computation.1 | async-start | bytes 3145728 | tf_op jit(solution)/shard_map/all_to_all | solution.py:53
  43.3 36.1 %all-to-all-done.1 = f32[16,1,16,1440]{3,2,1,0:T(8,128)S(1)} async-done(((f32[16,1,16,1440]{3,2,1,0:T(8,128)}), f32[16,1,16,1440]{3,2,1,0:T(8,128)S(1)}, u32[]{:S(2)}, u32[]{:S(2)}) %all-to-all-start.1) | async-done | bytes 1474592 | tf_op jit(solution)/shard_map/all_to_all | solution.py:53
  79.6 4.1 %collective-permute-start = (f32[1,1,1440]{2,1,0:T(1,128)S(1)}, f32[1,1,1440]{2,1,0:T(1,128)S(1)}, u32[]{:S(2)}, u32[]{:S(2)}) collective-permute-start(f32[1,1,1440]{2,1,0:T(1,128)S(1)} %get-tuple-element.34), channel_id=1, source_target_pairs={{1,0},{2,1},{3,2},{4,3},{5,4},{6,5},{7,6},{8,7},{9,8},{10,9},{11,1... | collective-permute-start | bytes 17288 | tf_op jit(solution)/shard_map/ppermute | solution.py:23
  83.7 3.0 %collective-permute-start.1 = (f32[1,1,1440]{2,1,0:T(1,128)S(1)}, f32[1,1,1440]{2,1,0:T(1,128)S(1)}, u32[]{:S(2)}, u32[]{:S(2)}) collective-permute-start(f32[1,1,1440]{2,1,0:T(1,128)S(1)} %get-tuple-element.35), channel_id=1, source_target_pairs={{0,1},{1,2},{2,3},{3,4},{4,5},{5,6},{6,7},{7,8},{8,9},{9,10},{10,1... | collective-permute-start | bytes 17288 | tf_op jit(solution)/shard_map/ppermute | solution.py:20
  87.7 1.9 collective-permute-start.2
  89.6 5.7 %collective-permute-start.3 = (f32[1,1,1440]{2,1,0:T(1,128)S(1)}, f32[1,1,1440]{2,1,0:T(1,128)S(1)}, u32[]{:S(2)}, u32[]{:S(2)}) collective-permute-start(f32[1,1,1440]{2,1,0:T(1,128)S(1)} %get-tuple-element.29), channel_id=1, source_target_pairs={{0,1},{1,2},{2,3},{3,4},{4,5},{5,6},{6,7},{7,8},{8,9},{9,10},{10,1... | collective-permute-start | bytes 17288 | tf_op jit(solution)/shard_map/ppermute | solution.py:20
  97.1 41.8 %all_to_all.38 = f32[16,1,16,1440]{3,2,1,0:T(8,128)S(1)} all-to-all(f32[16,1,16,1440]{3,2,1,0:T(8,128)S(1)} %broadcast_in_dim.14), channel_id=1, replica_groups=mesh['tm'=16,'tile'=32] {'tm'}, dimensions={0} | all-to-all | bytes 2949120 | tf_op jit(solution)/shard_map/all_to_all | solution.py:30
  138.9 2.6 fusion.10
  142.0 20.6 %all_to_all.39 = f32[32,1,528]{2,1,0:T(1,128)S(1)} all-to-all(f32[32,1,528]{2,1,0:T(1,128)S(1)} %broadcast_in_dim.15), channel_id=1, replica_groups=mesh['tm'=16,'tile'=32] {'tile'}, dimensions={0} | all-to-all | bytes 135168 | tf_op jit(solution)/shard_map/all_to_all | solution.py:30
  165.4 40.0 %all_to_all.40 = f32[16,1,16,1440]{3,2,1,0:T(8,128)S(1)} all-to-all(f32[16,1,16,1440]{3,2,1,0:T(8,128)S(1)} %copy.59), channel_id=1, replica_groups=mesh['tm'=16,'tile'=32] {'tm'}, dimensions={0} | all-to-all | bytes 2949120 | tf_op jit(solution)/shard_map/all_to_all | solution.py:53
  205.7 4.7 %collective-permute-start.4 = (f32[1,1,1440]{2,1,0:T(1,128)S(1)}, f32[1,1,1440]{2,1,0:T(1,128)S(1)}, u32[]{:S(2)}, u32[]{:S(2)}) collective-permute-start(f32[1,1,1440]{2,1,0:T(1,128)S(1)} %get-tuple-element.22), channel_id=1, source_target_pairs={{1,0},{2,1},{3,2},{4,3},{5,4},{6,5},{7,6},{8,7},{9,8},{10,9},{11,1... | collective-permute-start | bytes 17288 | tf_op jit(solution)/shard_map/ppermute | solution.py:23
  210.4 2.8 collective-permute-start.5
  214.2 1.9 collective-permute-start.6
  216.1 5.7 %collective-permute-start.7 = (f32[1,1,1440]{2,1,0:T(1,128)S(1)}, f32[1,1,1440]{2,1,0:T(1,128)S(1)}, u32[]{:S(2)}, u32[]{:S(2)}) collective-permute-start(f32[1,1,1440]{2,1,0:T(1,128)S(1)} %get-tuple-element.17), channel_id=1, source_target_pairs={{0,1},{1,2},{2,3},{3,4},{4,5},{5,6},{6,7},{7,8},{8,9},{9,10},{10,1... | collective-permute-start | bytes 17288 | tf_op jit(solution)/shard_map/ppermute | solution.py:20
  223.5 41.5 %all_to_all.41 = f32[16,1,16,1440]{3,2,1,0:T(8,128)S(1)} all-to-all(f32[16,1,16,1440]{3,2,1,0:T(8,128)S(1)} %broadcast_in_dim.16), channel_id=1, replica_groups=mesh['tm'=16,'tile'=32] {'tm'}, dimensions={0} | all-to-all | bytes 2949120 | tf_op jit(solution)/shard_map/all_to_all | solution.py:30
  265.8 10.8 %all-to-all-start.6 = ((f32[32,1,16]{2,1,0:T(1,128)}), f32[32,1,16]{2,1,0:T(1,128)S(1)}, u32[]{:S(2)}, u32[]{:S(2)}) async-start(f32[32,1,16]{2,1,0:T(1,128)} %broadcast_in_dim.17), calls=%async_computation.6 | async-start | bytes 32768 | tf_op jit(solution)/shard_map/all_to_all | solution.py:30
  277.3 8.6 %all-to-all-done.6 = f32[32,1,16]{2,1,0:T(1,128)S(1)} async-done(((f32[32,1,16]{2,1,0:T(1,128)}), f32[32,1,16]{2,1,0:T(1,128)S(1)}, u32[]{:S(2)}, u32[]{:S(2)}) %all-to-all-start.6) | async-done | bytes 2080 | tf_op jit(solution)/shard_map/all_to_all | solution.py:30
  (66 shorter events, 15.0 us)
Async XLA Ops:
  2.0 16.3 %copy-start = (bf16[32,16,1440]{2,1,0:T(8,128)(2,1)S(1)}, bf16[32,16,1440]{2,1,0:T(8,128)(2,1)}, u32[]{:S(2)}) copy-start(bf16[32,16,1440]{2,1,0:T(8,128)(2,1)} %param.5) | copy-start | bytes 4423684
  7.1 21.2 %all-to-all-start = ((f32[32,1,528]{2,1,0:T(1,128)}), f32[32,1,528]{2,1,0:T(1,128)S(1)}, u32[]{:S(2)}, u32[]{:S(2)}) async-start(f32[32,1,528]{2,1,0:T(1,128)} %broadcast_in_dim.12), calls=%async_computation | async-start | bytes 163840 | tf_op jit(solution)/shard_map/all_to_all | solution.py:30
  32.3 10.3 %copy-start.4 = (f32[16]{0:T(128)S(1)}, f32[16]{0:T(128)}, u32[]{:S(2)}) copy-start(f32[16]{0:T(128)} %param.9) | copy-start | bytes 196
  32.3 47.1 %all-to-all-start.1 = ((f32[16,1,16,1440]{3,2,1,0:T(8,128)}), f32[16,1,16,1440]{3,2,1,0:T(8,128)S(1)}, u32[]{:S(2)}, u32[]{:S(2)}) async-start(f32[16,1,16,1440]{3,2,1,0:T(8,128)} %copy.52), calls=%async_computation.1 | async-start | bytes 3145728 | tf_op jit(solution)/shard_map/all_to_all | solution.py:53
  42.6 44.8 %copy-start.2 = (f32[16,1440]{1,0:T(8,128)S(1)}, f32[16,1440]{1,0:T(8,128)}, u32[]{:S(2)}) copy-start(f32[16,1440]{1,0:T(8,128)} %param.7) | copy-start | bytes 276484
  42.6 44.8 %copy-start.3 = (s32[16,1440]{1,0:T(8,128)S(1)}, s32[16,1440]{1,0:T(8,128)}, u32[]{:S(2)}) copy-start(s32[16,1440]{1,0:T(8,128)} %param.8) | copy-start | bytes 276484
  79.6 7.2 %collective-permute-start = (f32[1,1,1440]{2,1,0:T(1,128)S(1)}, f32[1,1,1440]{2,1,0:T(1,128)S(1)}, u32[]{:S(2)}, u32[]{:S(2)}) collective-permute-start(f32[1,1,1440]{2,1,0:T(1,128)S(1)} %get-tuple-element.34), channel_id=1, source_target_pairs={{1,0},{2,1},{3,2},{4,3},{5,4},{6,5},{7,6},{8,7},{9,8},{10,9},{11,1... | collective-permute-start | bytes 17288 | tf_op jit(solution)/shard_map/ppermute | solution.py:23
  83.7 3.7 %collective-permute-start.1 = (f32[1,1,1440]{2,1,0:T(1,128)S(1)}, f32[1,1,1440]{2,1,0:T(1,128)S(1)}, u32[]{:S(2)}, u32[]{:S(2)}) collective-permute-start(f32[1,1,1440]{2,1,0:T(1,128)S(1)} %get-tuple-element.35), channel_id=1, source_target_pairs={{0,1},{1,2},{2,3},{3,4},{4,5},{5,6},{6,7},{7,8},{8,9},{9,10},{10,1... | collective-permute-start | bytes 17288 | tf_op jit(solution)/shard_map/ppermute | solution.py:20
  87.7 7.7 %collective-permute-start.2 = (f32[1,1,1440]{2,1,0:T(1,128)S(1)}, f32[1,1,1440]{2,1,0:T(1,128)S(1)}, u32[]{:S(2)}, u32[]{:S(2)}) collective-permute-start(f32[1,1,1440]{2,1,0:T(1,128)S(1)} %get-tuple-element.28), channel_id=1, source_target_pairs={{1,0},{2,1},{3,2},{4,3},{5,4},{6,5},{7,6},{8,7},{9,8},{10,9},{11,1... | collective-permute-start | bytes 17288 | tf_op jit(solution)/shard_map/ppermute | solution.py:23
  89.6 6.5 %collective-permute-start.3 = (f32[1,1,1440]{2,1,0:T(1,128)S(1)}, f32[1,1,1440]{2,1,0:T(1,128)S(1)}, u32[]{:S(2)}, u32[]{:S(2)}) collective-permute-start(f32[1,1,1440]{2,1,0:T(1,128)S(1)} %get-tuple-element.29), channel_id=1, source_target_pairs={{0,1},{1,2},{2,3},{3,4},{4,5},{5,6},{6,7},{7,8},{8,9},{9,10},{10,1... | collective-permute-start | bytes 17288 | tf_op jit(solution)/shard_map/ppermute | solution.py:20
  97.1 41.9 %copy-start.1 = (bf16[32,16,1440]{2,1,0:T(8,128)(2,1)S(1)}, bf16[32,16,1440]{2,1,0:T(8,128)(2,1)}, u32[]{:S(2)}) copy-start(bf16[32,16,1440]{2,1,0:T(8,128)(2,1)} %param.5) | copy-start | bytes 4423684
  205.7 7.6 %collective-permute-start.4 = (f32[1,1,1440]{2,1,0:T(1,128)S(1)}, f32[1,1,1440]{2,1,0:T(1,128)S(1)}, u32[]{:S(2)}, u32[]{:S(2)}) collective-permute-start(f32[1,1,1440]{2,1,0:T(1,128)S(1)} %get-tuple-element.22), channel_id=1, source_target_pairs={{1,0},{2,1},{3,2},{4,3},{5,4},{6,5},{7,6},{8,7},{9,8},{10,9},{11,1... | collective-permute-start | bytes 17288 | tf_op jit(solution)/shard_map/ppermute | solution.py:23
  210.4 3.5 %collective-permute-start.5 = (f32[1,1,1440]{2,1,0:T(1,128)S(1)}, f32[1,1,1440]{2,1,0:T(1,128)S(1)}, u32[]{:S(2)}, u32[]{:S(2)}) collective-permute-start(f32[1,1,1440]{2,1,0:T(1,128)S(1)} %get-tuple-element.23), channel_id=1, source_target_pairs={{0,1},{1,2},{2,3},{3,4},{4,5},{5,6},{6,7},{7,8},{8,9},{9,10},{10,1... | collective-permute-start | bytes 17288 | tf_op jit(solution)/shard_map/ppermute | solution.py:20
  214.2 7.7 %collective-permute-start.6 = (f32[1,1,1440]{2,1,0:T(1,128)S(1)}, f32[1,1,1440]{2,1,0:T(1,128)S(1)}, u32[]{:S(2)}, u32[]{:S(2)}) collective-permute-start(f32[1,1,1440]{2,1,0:T(1,128)S(1)} %get-tuple-element.16), channel_id=1, source_target_pairs={{1,0},{2,1},{3,2},{4,3},{5,4},{6,5},{7,6},{8,7},{9,8},{10,9},{11,1... | collective-permute-start | bytes 17288 | tf_op jit(solution)/shard_map/ppermute | solution.py:23
  216.1 6.5 %collective-permute-start.7 = (f32[1,1,1440]{2,1,0:T(1,128)S(1)}, f32[1,1,1440]{2,1,0:T(1,128)S(1)}, u32[]{:S(2)}, u32[]{:S(2)}) collective-permute-start(f32[1,1,1440]{2,1,0:T(1,128)S(1)} %get-tuple-element.17), channel_id=1, source_target_pairs={{0,1},{1,2},{2,3},{3,4},{4,5},{5,6},{6,7},{7,8},{8,9},{9,10},{10,1... | collective-permute-start | bytes 17288 | tf_op jit(solution)/shard_map/ppermute | solution.py:20
  265.8 20.1 %all-to-all-start.6 = ((f32[32,1,16]{2,1,0:T(1,128)}), f32[32,1,16]{2,1,0:T(1,128)S(1)}, u32[]{:S(2)}, u32[]{:S(2)}) async-start(f32[32,1,16]{2,1,0:T(1,128)} %broadcast_in_dim.17), calls=%async_computation.6 | async-start | bytes 32768 | tf_op jit(solution)/shard_map/all_to_all | solution.py:30
where the time goes:
time: 288 us; the launch traced here: 287 us
  blocking collectives  144 us (50%)
  starting transfers between devices  62.1 us (22%)
  waiting for transfers between devices  52.6 us (18%)
  local copies, waits for them, and re-layouts  11.9 us (4%)
  matrix products  10.4 us (4%)
  other arithmetic  5.59 us (2%)
    all_to_all x3, blocking collectives, copy_for_each(): return lax.all_to_all(copies, axis, split_axis=0, concat_axis=0, tiled=True)  104 us
    all_to_all x1, blocking collectives, sent_and_summed(): lax.all_to_all(tiles, axis, split_axis=0, concat_axis=0, tiled=True)  40 us
    all_to_all x1, waiting for transfers between devices, sent_and_summed(): lax.all_to_all(tiles, axis, split_axis=0, concat_axis=0, tiled=True)  36.1 us
    all_to_all x2, starting transfers between devices, copy_for_each(): return lax.all_to_all(copies, axis, split_axis=0, concat_axis=0, tiled=True)  22 us
    ppermute x4, starting transfers between devices, extended(): lax.ppermute(lax.slice_in_dim(block, block.shape[dim] - width, None, axis...  17.2 us
    all_to_all x2, waiting for transfers between devices, copy_for_each(): return lax.all_to_all(copies, axis, split_axis=0, concat_axis=0, tiled=True)  13.8 us
    ppermute x4, starting transfers between devices, extended(): lax.ppermute(lax.slice_in_dim(block, 0, width, axis=dim), axis, backward)  12.6 us
    all_to_all x1, starting transfers between devices, sent_and_summed(): lax.all_to_all(tiles, axis, split_axis=0, concat_axis=0, tiled=True)  10.3 us
  transfers between devices with their start and end apart: 11, of which 7 were waited for; matrix products, arithmetic and copies ran while one was open for 2% of the time, Pallas kernels for 0%

commit v1 on v0

v1 whole, which is shorter than its diff:
```python
import functools
import math

import jax
import jax.numpy as jnp
from jax import lax
from jax.experimental import pallas as pl
from jax.experimental.pallas import tpu as pltpu
from jax.sharding import PartitionSpec as P

ITERS = 2
EPS = 1e-06
SHRINK = 0.2
MESH = pl.DeviceIdType.MESH
F32 = jnp.float32
BF16 = jnp.bfloat16


def iota(shape, dim):
    return lax.broadcasted_iota(jnp.int32, shape, dim)


def kernel(
    geo,
    anom_hbm,
    init_hbm,
    diff_hbm,
    land_hbm,
    thr_ref,
    cur_out,
    sc_out,
    anom,
    init,
    diff,
    land,
    pa,
    pb,
    ga,
    gb,
    xb,
    xa,
    zr,
    s1,
    s2,
    hs,
    hr,
    ds,
    dr,
    field,
    dcoef,
    ncoef,
    scoef,
    sval,
    load_sem,
    z_s,
    z_r,
    x_s,
    x_r,
    g_s,
    g_r,
    y_s,
    y_r,
    a1_s,
    a1_r,
    a2_s,
    a2_r,
    h_s,
    h_r,
    d_s,
    d_r,
):
    nz, ny, lat_rows, lon, lat_total = geo
    cells = lat_total * lon
    ntile = ny * 4
    tm = lax.axis_index("tm")
    tile = lax.axis_index("tile")
    u = lax.div(tm, nz)
    z = lax.rem(tm, nz)
    v = 1 - u
    core = lax.rem(tile, 2)
    xh = lax.rem(lax.div(tile, 2), 2)
    y = lax.div(tile, 4)
    sg = 1 - 2 * core

    def zat(steps):
        return lax.rem(z + steps * sg + 2 * nz, nz)

    nl = nz // 2
    ns = nl - 1
    plus = {"tm": u * nz + zat(1)}
    minus = {"tm": u * nz + zat(-1)}
    across = {"tm": v * nz + z}
    below = {"tile": lax.rem(tile + ntile - 1, ntile)}
    above = {"tile": lax.rem(tile + 1, ntile)}
    quad = []
    for dx, dc in ((0, 1), (1, 0), (1, 1)):
        px = lax.rem(xh + dx, 2)
        pc = lax.rem(core + dc, 2)
        quad.append((px * 2 + pc, {"tile": y * 4 + px * 2 + pc}))
    column = []
    for dy in range(1, ny):
        to = lax.rem(y + dy, ny)
        frm = lax.rem(y + ny - dy, ny)
        column.append((frm, {"tile": to * 4 + xh * 2 + core}))

    loads = [
        pltpu.make_async_copy(init_hbm, init, load_sem.at[0]),
        pltpu.make_async_copy(anom_hbm, anom, load_sem.at[1]),
        pltpu.make_async_copy(diff_hbm, diff, load_sem.at[2]),
        pltpu.make_async_copy(land_hbm, land, load_sem.at[3]),
    ]
    for copy in loads:
        copy.start()

    barrier = pltpu.get_barrier_semaphore()
    peers = [plus, minus, across, below, above] + [d for _, d in quad] + [d for _, d in column]
    for peer in peers:
        pl.semaphore_signal(barrier, inc=1, device_id=peer, device_id_type=MESH)

    def remote(src, dst, send, recv, where):
        return pltpu.make_async_remote_copy(
            src_ref=src, dst_ref=dst, send_sem=send, recv_sem=recv, device_id=where, device_id_type=MESH
        )

    modes = 2 * nz
    rows = modes * 8
    c_col = iota((rows, 128), 0)
    lane = iota((rows, 128), 1)
    mode_of = lax.rem(lax.div(c_col, 8), 2) * nz + lax.div(c_col, 16)

    loads[2].wait()
    loads[3].wait()
    dcoef[...] = jnp.zeros_like(dcoef)
    diffuse = diff[...] * (1.0 + land[...].astype(F32)) * 0.5
    dcoef[8:24, :lon] = diffuse
    ds[0] = diffuse[0:2]
    ds[1] = diffuse[14:16]
    row_index = (tile * lat_rows + iota((32, 128), 0) - 8).astype(F32)
    centre = jnp.sin(jnp.pi * (row_index + 0.5) / lat_total)
    ncoef[...] = SHRINK * jnp.sin(jnp.pi * (row_index + 1.0) / lat_total) / centre
    scoef[...] = SHRINK * jnp.sin(jnp.pi * row_index / lat_total) / centre

    loads[0].wait()
    for m in range(modes):
        wide = init[m].astype(F32)
        ga[m % nz, m // nz] = wide[0:8]
        gb[m % nz, m // nz] = wide[8:16]
    loads[1].wait()

    pl.semaphore_wait(barrier, len(peers))
    d_copies = [
        remote(ds.at[0], dr.at[1], d_s.at[0], d_r.at[1], below),
        remote(ds.at[1], dr.at[0], d_s.at[1], d_r.at[0], above),
    ]
    for copy in d_copies:
        copy.start()

    def square_row():
        a = ga[...].reshape(rows, lon)
        b = gb[...].reshape(rows, lon)
        total = jnp.sum(a * a + b * b, axis=1, keepdims=True)
        spread = jnp.where((lane >= 64) & (lax.rem(lane, 16) == mode_of), total, 0.0)
        return jnp.sum(spread, axis=0, keepdims=True)

    def over_tile(at, message):
        me = xh * 2 + core
        s1[at, me] = message
        first = [
            remote(s1.at[at, me], s1.at[at, me], a1_s.at[at, j], a1_r.at[at, j], where)
            for j, (_, where) in enumerate(quad)
        ]
        for copy in first:
            copy.start()
        for j, (slot, where) in enumerate(quad):
            remote(s1.at[at, slot], s1.at[at, slot], a1_s.at[at, j], a1_r.at[at, j], where).wait_recv()
        s2[at, y] = (s1[at, 0] + s1[at, 1]) + (s1[at, 2] + s1[at, 3])
        second = [
            remote(s2.at[at, y], s2.at[at, y], a2_s.at[at, j], a2_r.at[at, j], where)
            for j, (_, where) in enumerate(column)
        ]
        for copy in second:
            copy.start()
        for j, (slot, where) in enumerate(column):
            remote(s2.at[at, slot], s2.at[at, slot], a2_s.at[at, j], a2_r.at[at, j], where).wait_recv()
        total = s2[at, 0]
        for j in range(1, ny):
            total = total + s2[at, j]
        for copy in first + second:
            copy.wait_send()
        return total

    def step(it, _):
        half_a = ga[...].reshape(rows, lon)
        half_b = gb[...].reshape(rows, lon)
        rounded = jnp.concatenate([half_a, half_b], axis=0).astype(BF16)
        product = lax.dot_general(anom[...], rounded, (((1,), (1,)), ((), ())), preferred_element_type=F32)
        times = anom.shape[0] // 16
        prod_a = product[:, :rows].reshape(times, 2, 8, rows)
        prod_b = product[:, rows:].reshape(times, 2, 8, rows)
        same = lax.rem(iota((8, rows), 1), 8) == iota((8, rows), 0)
        kept = jnp.where(same, prod_a[:, 0] + prod_b[:, 1], 0.0)
        by_row = jnp.sum(kept, axis=1)
        message = jnp.broadcast_to(square_row(), (8, 128))
        for b in range(4):
            pick = jnp.where(lane == b * 16 + mode_of, 1.0, 0.0).astype(F32)
            message = message + lax.dot_general(
                by_row[b * 8 : (b + 1) * 8],
                pick,
                (((1,), (0,)), ((), ())),
                precision=lax.Precision.HIGHEST,
                preferred_element_type=F32,
            )
        total = over_tile(it, message)
        factor = lax.rsqrt(pltpu.roll(total, 64, 1) / cells + EPS)
        scores = total * factor / math.sqrt(cells)
        scores = jnp.where(iota((8, 128), 1) < 64, scores, 0.0)
        sval[...] = scores

        tall = jnp.broadcast_to(scores.reshape(8, 1, 128), (8, 16, 128)).reshape(128, 128)
        tall = tall.T.astype(BF16)
        left = []
        for b in range(4):
            pick = jnp.where(lane == b * 16 + mode_of, 1.0, 0.0).astype(BF16)
            wide = jnp.dot(pick, tall, preferred_element_type=F32)
            at_a = lax.rem(lane, 16) == lax.rem(c_col, 8)
            at_b = lax.rem(lane, 16) == lax.rem(c_col, 8) + 8
            left.append(jnp.concatenate([jnp.where(at_a, wide, 0.0), jnp.where(at_b, wide, 0.0)], axis=0).astype(BF16))
        spread = jnp.concatenate(left, axis=1)
        part = jnp.dot(spread, anom[...], preferred_element_type=F32)
        pb[...] = part[rows:].reshape(nz, 2, 8, lon)
        pa[...] = part[:rows].reshape(nz, 2, 8, lon)

        sent = []

        def go(copy):
            copy.start()
            sent.append(copy)

        offsets = [nl]
        for r in range(ns, 0, -1):
            offsets += [-r, r]
        offsets += [0]
        place = {off: q for q, off in enumerate(offsets)}
        x_in = [remote(pb.at[zat(off), v], xb.at[q], x_s.at[q], x_r.at[q], across) for q, off in enumerate(offsets)]

        def own(c, off):
            if c == 0:
                return pa.at[zat(off), v]
            if c == 1:
                return pa.at[zat(off), u]
            return xb.at[place[off]]

        def prepare(off):
            q = place[off]
            x_in[q].wait_recv()
            xb[q] = xb[q] + pb[zat(off), u]

        def z_copy(c, r, long):
            slot = r if long else nl + r
            top = nl if long else ns
            if r == top - 1:
                src = own(c, top if long else -top)
            else:
                src = zr.at[c, slot + 1]
            return remote(src, zr.at[c, slot], z_s.at[c, slot], z_r.at[c, slot], plus if long else minus)

        for copy in x_in:
            go(copy)
        for c in (0, 1):
            go(z_copy(c, nl - 1, True))
            go(z_copy(c, ns - 1, False))
        prepare(nl)
        go(z_copy(2, nl - 1, True))
        prepare(-ns)
        go(z_copy(2, ns - 1, False))
        for r in range(nl - 1, 0, -1):
            for c in (0, 1, 2):
                if c == 2:
                    prepare(r)
                z_copy(c, r, True).wait_recv()
                zr[c, r] = zr[c, r] + own(c, r)[...]
                go(z_copy(c, r - 1, True))
                q = r - 1
                if q > 0:
                    if c == 2:
                        prepare(-q)
                    z_copy(c, q, False).wait_recv()
                    zr[c, nl + q] = zr[c, nl + q] + own(c, -q)[...]
                    go(z_copy(c, q - 1, False))
        prepare(0)

        def last(c):
            z_copy(c, 0, False).wait_recv()
            z_copy(c, 0, True).wait_recv()
            return own(c, 0)[...] + zr[c, 0] + zr[c, nl]

        xa[0] = last(0)
        x_last = remote(xa.at[0], xa.at[1], x_s.at[nz], x_r.at[nz], across)
        go(x_last)
        mine = last(1)
        sum_b = last(2)
        hs[1] = sum_b[6:8]
        h_up = remote(hs.at[1], hr.at[0], h_s.at[1], h_r.at[0], above)
        go(h_up)
        x_last.wait_recv()
        sum_a = mine + xa[1]
        hs[0] = sum_a[0:2]
        h_down = remote(hs.at[0], hr.at[1], h_s.at[0], h_r.at[1], below)
        go(h_down)

        width = field.shape[1]
        col = iota((32, width), 1)

        def wrapped(values):
            right = pltpu.roll(values, lon, 1)
            left = pltpu.roll(values, width - lon, 1)
            return jnp.where(col < lon, values, jnp.where(col < (lon + width) // 2, right, left))

        @pl.when(it == 0)
        def _():
            for copy in d_copies:
                copy.wait_recv()
            dcoef[6:8, :lon] = dr[0]
            dcoef[24:26, :lon] = dr[1]
            dcoef[...] = wrapped(dcoef[...])

        field[8:16, :lon] = sum_a
        field[16:24, :lon] = sum_b
        h_up.wait_recv()
        h_down.wait_recv()
        field[6:8, :lon] = hr[0]
        field[24:26, :lon] = hr[1]
        local_row = iota((32, width), 0) - 8
        global_row = local_row + tile * lat_rows
        inside = (global_row >= 0) & (global_row < lat_total) & (local_row >= -2) & (local_row < 18)
        f = jnp.where(inside, wrapped(field[...]), 0.0)
        north = ncoef[:, 0:1]
        south = scoef[:, 0:1]
        for _pass in range(2):
            east = pltpu.roll(f, width - 1, 1)
            west = pltpu.roll(f, 1, 1)
            upper = pltpu.roll(f, 31, 0)
            lower = pltpu.roll(f, 1, 0)
            change = SHRINK * (east + west - 2.0 * f) + north * (upper - f) + south * (lower - f)
            f = jnp.where(inside, f + dcoef[...] * change, 0.0)
        smoothed = f[8:24, :lon]
        shrunk = jnp.maximum(jnp.abs(smoothed) - thr_ref[tm], 0.0)
        pruned = jnp.where(smoothed < 0.0, -shrunk, shrunk)
        ga[z, u] = pruned[0:8]
        gb[z, u] = pruned[8:16]

        def g_ref(c, off):
            if c == 0:
                return ga.at[zat(off), u]
            if c == 1:
                return gb.at[zat(off), u]
            return ga.at[zat(off), v]

        def g_copy(c, h, long):
            ref = g_ref(c, 1 - h if long else h - 1)
            slot = h - 1 if long else nl + h - 1
            return remote(ref, ref, g_s.at[c, slot], g_r.at[c, slot], plus if long else minus)

        def g_wait(c, h, long):
            ref = g_ref(c, -h if long else h)
            slot = h - 1 if long else nl + h - 1
            remote(ref, ref, g_s.at[c, slot], g_r.at[c, slot], plus if long else minus).wait_recv()

        def y_copy(q, off):
            ref = gb.at[zat(off), u]
            return remote(ref, ref, y_s.at[q], y_r.at[q], across)

        while sent:
            sent.pop().wait_send()
        a_mine = ga.at[z, u]
        go(remote(a_mine, a_mine, y_s.at[nz], y_r.at[nz], across))
        for c in (0, 1):
            go(g_copy(c, 1, True))
            go(g_copy(c, 1, False))
        go(y_copy(0, 0))
        a_other = ga.at[z, v]
        remote(a_other, a_other, y_s.at[nz], y_r.at[nz], across).wait_recv()
        go(g_copy(2, 1, True))
        go(g_copy(2, 1, False))
        queue = [0]
        for h in range(1, nl + 1):
            for c in (0, 1, 2):
                g_wait(c, h, True)
                if h < nl:
                    go(g_copy(c, h + 1, True))
                if c == 1:
                    go(y_copy(len(queue), -h))
                    queue.append(-h)
                if h <= ns:
                    g_wait(c, h, False)
                    if h < ns:
                        go(g_copy(c, h + 1, False))
                    if c == 1:
                        go(y_copy(len(queue), h))
                        queue.append(h)
        for q, off in enumerate(queue):
            ref = gb.at[zat(off), v]
            remote(ref, ref, y_s.at[q], y_r.at[q], across).wait_recv()
        for copy in sent:
            copy.wait_send()
        return 0

    lax.fori_loop(0, ITERS, step, 0)
    for copy in d_copies:
        copy.wait_send()

    total = over_tile(ITERS, jnp.broadcast_to(square_row(), (8, 128)))
    factor = lax.rsqrt(total / cells + EPS)
    picked = jnp.where(lane == 64 + mode_of, jnp.broadcast_to(factor[0:1], (rows, 128)), 0.0)
    column_factor = jnp.sum(picked, axis=1, keepdims=True)
    out_a = ga[...].reshape(rows, lon) * column_factor
    out_b = gb[...].reshape(rows, lon) * column_factor
    for m in range(modes):
        c = (m % nz) * 16 + (m // nz) * 8
        cur_out[m, 0:8] = out_a[c : c + 8]
        cur_out[m, 8:16] = out_b[c : c + 8]
    for b in range(4):
        moved = sval[...] if b == 0 else pltpu.roll(sval[...], 128 - 16 * b, 1)
        sc_out[b * 8 : (b + 1) * 8, :] = moved[:, :16]


def solution(mesh):
    nz = mesh.shape["tm"] // 2
    ny = mesh.shape["tile"] // 4

    def local(anomalies, initial, diffusivity, land_mask, threshold):
        times, lat_rows, lon = anomalies.shape
        modes = initial.shape[0]
        lat_total = lat_rows * mesh.shape["tile"]
        width = (lon + 127) // 128 * 128
        vmem = pltpu.VMEM
        dma = pltpu.SemaphoreType.DMA
        any_space = pl.BlockSpec(memory_space=pl.ANY)
        in_vmem = pl.BlockSpec(memory_space=pltpu.VMEM)
        half = (nz, 2, 8, lon)
        return pl.pallas_call(
            functools.partial(kernel, (nz, ny, lat_rows, lon, lat_total)),
            out_shape=(
                jax.ShapeDtypeStruct((modes, lat_rows, lon), F32),
                jax.ShapeDtypeStruct((times, modes), F32),
            ),
            in_specs=[any_space] * 4 + [pl.BlockSpec(memory_space=pltpu.SMEM)],
            out_specs=(in_vmem, in_vmem),
            scratch_shapes=[
                vmem((times * lat_rows, lon), BF16),
                vmem((modes, lat_rows, lon), BF16),
                vmem((lat_rows, lon), F32),
                vmem((lat_rows, lon), jnp.int32),
                vmem(half, F32),
                vmem(half, F32),
                vmem(half, F32),
                vmem(half, F32),
                vmem((nz, 8, lon), F32),
                vmem((2, 8, lon), F32),
                vmem((3, nz - 1, 8, lon), F32),
                vmem((ITERS + 1, 4, 8, 128), F32),
                vmem((ITERS + 1, ny, 8, 128), F32),
                vmem((2, 2, lon), F32),
                vmem((2, 2, lon), F32),
                vmem((2, 2, lon), F32),
                vmem((2, 2, lon), F32),
                vmem((32, width), F32),
                vmem((32, width), F32),
                vmem((32, 128), F32),
                vmem((32, 128), F32),
                vmem((8, 128), F32),
                dma((4,)),
                dma((3, nz - 1)),
                dma((3, nz - 1)),
                dma((nz + 1,)),
                dma((nz + 1,)),
                dma((3, nz - 1)),
                dma((3, nz - 1)),
                dma((nz + 1,)),
                dma((nz + 1,)),
                dma((ITERS + 1, 3)),
                dma((ITERS + 1, 3)),
                dma((ITERS + 1, ny - 1)),
                dma((ITERS + 1, ny - 1)),
                dma((2,)),
                dma((2,)),
                dma((2,)),
                dma((2,)),
            ],
            compiler_params=pltpu.CompilerParams(
                collective_id=0, has_side_effects=True, vmem_limit_bytes=48 * 1024 * 1024
            ),
        )(anomalies.reshape(times * lat_rows, lon), initial, diffusivity, land_mask, threshold)

    return jax.shard_map(
        local,
        mesh=mesh,
        in_specs=(
            P("tm", "tile", None),
            P(None, "tile", None),
            P("tile", None),
            P("tile", None),
            P(),
        ),
        out_specs=(P(None, "tile", None), P("tm", None)),
        check_vma=False,
    )
```

time: 288 us -> 132 us (0.46)
  blocking collectives: 144 us -> 0 us
  Pallas kernels: 0 us -> 124 us
  starting transfers between devices: 62.1 us -> 0 us
  waiting for transfers between devices: 52.6 us -> 0 us
  matrix products: 10.4 us -> 0 us
  other arithmetic: 5.59 us -> 0 us
  local copies, waits for them, and re-layouts: 11.9 us -> 6.78 us
    all_to_all x4 -> x0, blocking collectives: 144 us -> none  [the longest x3 104 us: copy_for_each(): return lax.all_to_all(copies, axis, split_axis=0, concat_axis=0, tiled=True)]
    pallas_call x0 -> x1, Pallas kernels: none -> 124 us  [local(): pl.pallas_call(functools.partial(kernel, (nz, ny, lat_rows, lon, lat_tota...]
    all_to_all x3 -> x0, waiting for transfers between devices: 49.9 us -> none  [the longest x1 36.1 us: sent_and_summed(): lax.all_to_all(tiles, axis, split_axis=0, concat_axis=0, tiled=True)]
    all_to_all x3 -> x0, starting transfers between devices: 32.3 us -> none  [the longest x2 22 us: copy_for_each(): return lax.all_to_all(copies, axis, split_axis=0, concat_axis=0, tiled=True)]
    ppermute x8 -> x0, starting transfers between devices: 29.8 us -> none  [the longest x4 17.2 us: extended(): lax.ppermute(lax.slice_in_dim(block, block.shape[dim] - width, None, axis...]
    dot_general x4 -> x0, matrix products: 10.4 us -> none  [the longest x2 6.84 us: local(): lax.dot_general(flattened, rounded.reshape(mode_count, lat_rows * lon_cel...]
    unnamed x11, local copies, waits for them, and re-layouts: 0.7 us -> 6.11 us
    dot_general x3 -> x0, local copies, waits for them, and re-layouts: 3.05 us -> none  [the longest x2 2.97 us: local(): lax.dot_general(scores.astype(jnp.bfloat16), flattened, (((0,), (0,)), ((...]
  transfers between devices with their start and end apart: 11 -> 0, of which waited for: 7 -> 0; matrix products, arithmetic and copies ran while one was open for 2% -> 0% of each run, Pallas kernels for 0% -> 0%
where the time goes in v1:
time: 132 us
  Pallas kernels  124 us (94%)
  local copies, waits for them, and re-layouts  6.78 us (5%)
    pallas_call x1, Pallas kernels, local(): pl.pallas_call(functools.partial(kernel, (nz, ny, lat_rows, lon, lat_tota...  124 us
    unnamed x11, local copies, waits for them, and re-layouts  6.11 us

profile of v1, /device:TPU:1, one launch (start us, length us, event | category | flops | bytes accessed | tf_op | source)
XLA Modules:
  0.0 131.7 jit_solution(3788119072174562428)
XLA Ops:
  0.6 0.0 copy-start
  0.6 1.4 %copy-done = bf16[32,16,1440]{2,1,0:T(8,128)(2,1)S(1)} copy-done((bf16[32,16,1440]{2,1,0:T(8,128)(2,1)S(1)}, bf16[32,16,1440]{2,1,0:T(8,128)(2,1)}, u32[]{:S(2)}) %copy-start) | copy-done | bytes 1474584
  2.0 0.0 copy-start.1
  2.0 1.1 copy-done.1
  3.2 0.0 copy-start.2
  3.2 0.9 copy-done.2
  4.1 0.0 copy-start.3
  4.1 0.9 copy-done.3
  5.0 0.0 copy-start.4
  5.0 0.7 copy-done.4
  5.6 124.3 %shard_map.68 = (f32[16,16,1440]{2,1,0:T(8,128)S(1)}, f32[32,16]{1,0:T(8,128)S(1)}) custom-call(bf16[512,1440]{1,0:T(8,128)(2,1)S(1)} %bitcast.1, bf16[16,16,1440]{2,1,0:T(8,128)(2,1)S(1)} %copy-done.1, f32[16,1440]{1,0:T(8,128)S(1)} %copy-done.2, s32[16,1440]{1,0:T(8,128)S(1)} %copy-done.3, f32[16]{0:T(128)S(1)} %copy-done.4), custom_call_target="tpu_custom_call" | custom-call | tf_op jit(solution)/shard_map/pallas_call | solution.py:441
  129.9 0.7 copy.7
  130.6 1.1 copy.9
Async XLA Ops:
  0.6 1.4 %copy-start = (bf16[32,16,1440]{2,1,0:T(8,128)(2,1)S(1)}, bf16[32,16,1440]{2,1,0:T(8,128)(2,1)}, u32[]{:S(2)}) copy-start(bf16[32,16,1440]{2,1,0:T(8,128)(2,1)} %param.5) | copy-start | bytes 4423684
  2.0 1.1 copy-start.1
  3.2 0.9 copy-start.2
  4.1 0.9 copy-start.3
  5.0 0.7 copy-start.4

commit v2 on v1

v2 whole, which is shorter than its diff:
```python
import functools
import math

import jax
import jax.numpy as jnp
from jax import lax
from jax.experimental import pallas as pl
from jax.experimental.pallas import tpu as pltpu
from jax.sharding import PartitionSpec as P

ITERS = 2
EPS = 1e-06
SHRINK = 0.2
MESH = pl.DeviceIdType.MESH
F32 = jnp.float32
BF16 = jnp.bfloat16


def iota(shape, dim):
    return lax.broadcasted_iota(jnp.int32, shape, dim)


def kernel(
    geo,
    anom_hbm,
    init_hbm,
    diff_hbm,
    land_hbm,
    thr_hbm,
    cur_out,
    sc_out,
    anom,
    init,
    diff,
    land,
    thr_ref,
    pa,
    pb,
    ga,
    gb,
    xb,
    xa,
    zr,
    s1,
    s2,
    fr,
    hs,
    hr,
    ds,
    dr,
    field,
    dcoef,
    ncoef,
    scoef,
    sval,
    fac,
    msg,
    load_sem,
    z_s,
    z_r,
    x_s,
    x_r,
    g_s,
    g_r,
    y_s,
    y_r,
    a1_s,
    a1_r,
    a2_s,
    a2_r,
    f_s,
    f_r,
    h_s,
    h_r,
    d_s,
    d_r,
):
    nz, ny, lat_rows, lon, lat_total = geo
    cells = lat_total * lon
    ntile = ny * 4
    tm = lax.axis_index("tm")
    tile = lax.axis_index("tile")
    u = lax.div(tm, nz)
    z = lax.rem(tm, nz)
    v = 1 - u
    core = lax.rem(tile, 2)
    xh = lax.rem(lax.div(tile, 2), 2)
    y = lax.div(tile, 4)
    sg = 1 - 2 * core

    def zat(steps):
        return lax.rem(z + steps * sg + 2 * nz, nz)

    plus = {"tm": u * nz + zat(1)}
    plus2 = {"tm": u * nz + zat(2)}
    minus = {"tm": u * nz + zat(-1)}
    minus2 = {"tm": u * nz + zat(-2)}
    across = {"tm": v * nz + z}
    below = {"tile": lax.rem(tile + ntile - 1, ntile)}
    above = {"tile": lax.rem(tile + 1, ntile)}
    mate = {"tile": tile + sg}
    spread_to = []
    for dy in sorted(range(ny), key=lambda d: -min(d, ny - d)):
        for dx in (1, 0):
            if dy or dx:
                ox = lax.rem(xh + dx, 2)
                to = lax.rem(y + dy, ny)
                frm = lax.rem(y + ny - dy, ny)
                spread_to.append((frm * 2 + ox, {"tile": to * 4 + ox * 2 + core}))
    factor_to = []
    for dz in sorted(range(nz), key=lambda d: -min(d, nz - d)):
        for du in (1, 0):
            if dz or du:
                ou = lax.rem(u + du, 2)
                to = lax.rem(z + dz, nz)
                frm = lax.rem(z + nz - dz, nz)
                factor_to.append((ou * nz + frm, {"tm": ou * nz + to}))

    loads = [
        pltpu.make_async_copy(init_hbm, init, load_sem.at[0]),
        pltpu.make_async_copy(anom_hbm, anom, load_sem.at[1]),
        pltpu.make_async_copy(diff_hbm, diff, load_sem.at[2]),
        pltpu.make_async_copy(land_hbm, land, load_sem.at[3]),
        pltpu.make_async_copy(thr_hbm, thr_ref, load_sem.at[4]),
    ]
    for copy in loads:
        copy.start()

    barrier = pltpu.get_barrier_semaphore()
    peers = [below, above, mate] + [d for _, d in spread_to] + [d for _, d in factor_to]
    for peer in peers:
        pl.semaphore_signal(barrier, inc=1, device_id=peer, device_id_type=MESH)

    def remote(src, dst, send, recv, where):
        return pltpu.make_async_remote_copy(
            src_ref=src, dst_ref=dst, send_sem=send, recv_sem=recv, device_id=where, device_id_type=MESH
        )

    modes = 2 * nz
    rows = modes * 8
    c_col = iota((rows, 128), 0)
    lane = iota((rows, 128), 1)
    mode_of = lax.rem(lax.div(c_col, 8), 2) * nz + lax.div(c_col, 16)

    def row_in_band(i):
        return i + 4, jnp.where(i < 4, i, i + 8)

    loads[2].wait()
    loads[3].wait()
    dcoef[...] = jnp.zeros_like(dcoef)
    diffuse = diff[...] * (1.0 + land[...].astype(F32)) * 0.5
    dcoef[8:24, :lon] = diffuse
    ds[0] = diffuse[0:2]
    ds[1] = diffuse[14:16]
    row_index = (tile * lat_rows + iota((32, 128), 0) - 8).astype(F32)
    centre = jnp.sin(jnp.pi * (row_index + 0.5) / lat_total)
    ncoef[...] = SHRINK * jnp.sin(jnp.pi * (row_index + 1.0) / lat_total) / centre
    scoef[...] = SHRINK * jnp.sin(jnp.pi * row_index / lat_total) / centre

    loads[0].wait()
    for m in range(modes):
        wide = init[m].astype(F32)
        ga[m % nz, m // nz] = wide[4:12]
        gb[m % nz, m // nz] = jnp.concatenate([wide[0:4], wide[12:16]], axis=0)
    loads[1].wait()
    loads[4].wait()

    def square_row():
        a = ga[...].reshape(rows, lon)
        b = gb[...].reshape(rows, lon)
        total = jnp.sum(a * a + b * b, axis=1, keepdims=True)
        spread = jnp.where((lane >= 64) & (lax.rem(lane, 16) == mode_of), total, 0.0)
        return jnp.sum(spread, axis=0, keepdims=True)

    def partial_scores():
        half_a = ga[...].reshape(rows, lon)
        half_b = gb[...].reshape(rows, lon)
        rounded = jnp.concatenate([half_a, half_b], axis=0).astype(BF16)
        product = lax.dot_general(anom[...], rounded, (((1,), (1,)), ((), ())), preferred_element_type=F32)
        times = anom.shape[0] // 16
        prod_a = product[:, :rows].reshape(times, 16, rows)
        prod_b = product[:, rows:].reshape(times, 16, rows)
        here = iota((16, rows), 0)
        in_a, in_b = row_in_band(lax.rem(iota((16, rows), 1), 8))
        kept = jnp.where(here == in_a, prod_a, 0.0) + jnp.where(here == in_b, prod_b, 0.0)
        by_row = jnp.sum(kept, axis=1)
        message = jnp.zeros((8, 128), F32)
        for b in range(4):
            pick = jnp.where(lane == b * 16 + mode_of, 1.0, 0.0).astype(F32)
            message = message + lax.dot_general(
                by_row[b * 8 : (b + 1) * 8],
                pick,
                (((1,), (0,)), ((), ())),
                precision=lax.Precision.HIGHEST,
                preferred_element_type=F32,
            )
        return message

    msg[...] = partial_scores() + square_row()

    pl.semaphore_wait(barrier, len(peers))
    d_copies = [
        remote(ds.at[0], dr.at[1], d_s.at[0], d_r.at[1], below),
        remote(ds.at[1], dr.at[0], d_s.at[1], d_r.at[0], above),
    ]
    for copy in d_copies:
        copy.start()

    def step(it, _):
        late = []

        def go(copy, waits):
            copy.start()
            waits.append(copy)

        def tile_first(at, message):
            s1[at, core] = message
            go(remote(s1.at[at, core], s1.at[at, core], a1_s.at[at], a1_r.at[at], mate), late)

        def tile_second(at):
            other = s1.at[at, 1 - core]
            remote(other, other, a1_s.at[at], a1_r.at[at], mate).wait_recv()
            me = y * 2 + xh
            s2[at, me] = s1[at, 0] + s1[at, 1]
            for j, (_, where) in enumerate(spread_to):
                go(remote(s2.at[at, me], s2.at[at, me], a2_s.at[at, j], a2_r.at[at, j], where), late)

        def tile_total(at):
            for j, (slot, where) in enumerate(spread_to):
                remote(s2.at[at, slot], s2.at[at, slot], a2_s.at[at, j], a2_r.at[at, j], where).wait_recv()
            return jnp.sum(s2[at], axis=0)

        tile_first(it, msg[...])
        tile_second(it)
        total = tile_total(it)

        @pl.when(it == 0)
        def _():
            fac[...] = lax.rsqrt(pltpu.roll(total, 64, 1) / cells + EPS)

        scores = total * fac[...] / math.sqrt(cells)
        scores = jnp.where(iota((8, 128), 1) < 64, scores, 0.0)
        sval[...] = scores

        tall = jnp.broadcast_to(scores.reshape(8, 1, 128), (8, 16, 128)).reshape(128, 128)
        tall = tall.T.astype(BF16)
        left = []
        for b in range(4):
            pick = jnp.where(lane == b * 16 + mode_of, 1.0, 0.0).astype(BF16)
            wide = jnp.dot(pick, tall, preferred_element_type=F32)
            in_a, in_b = row_in_band(lax.rem(c_col, 8))
            here = lax.rem(lane, 16)
            left.append(
                jnp.concatenate([jnp.where(here == in_a, wide, 0.0), jnp.where(here == in_b, wide, 0.0)], axis=0).astype(BF16)
            )
        spread = jnp.concatenate(left, axis=1)
        part = jnp.dot(spread, anom[...], preferred_element_type=F32)
        pb[...] = part[rows:].reshape(nz, 2, 8, lon)
        pa[...] = part[:rows].reshape(nz, 2, 8, lon)

        early = []
        offsets = (4, 3, -3, 2, -2, 1, -1, 0)
        place = {off: q for q, off in enumerate(offsets)}
        x_in = [remote(pb.at[zat(off), v], xb.at[q], x_s.at[q], x_r.at[q], across) for q, off in enumerate(offsets)]
        slots = {4: 0, 3: 1, 2: 2, 1: 3, -3: 4, -2: 5, -1: 6}

        def own(c, off):
            if c == 0:
                return pa.at[zat(off), v]
            if c == 1:
                return pa.at[zat(off), u]
            return xb.at[place[off]]

        def prepare(c, off):
            if c == 2:
                q = place[off]
                x_in[q].wait_recv()
                xb[q] = xb[q] + pb[zat(off), u]

        def z_copy(c, off):
            slot = slots[off]
            if off in (4, 3, -3):
                src = own(c, off)
            else:
                src = zr.at[c, {2: 0, 1: 2, -2: 4, -1: 5}[off]]
            where = plus2 if off == 4 else plus if off > 0 else minus
            return remote(src, zr.at[c, slot], z_s.at[c, slot], z_r.at[c, slot], where)

        for copy in x_in[:3]:
            go(copy, late)
        for c in (0, 1):
            for off in (4, 3, -3):
                go(z_copy(c, off), early)
        for copy in x_in[3:]:
            go(copy, late)
        for off in (4, 3, -3):
            prepare(2, off)
            go(z_copy(2, off), early)
        for c in (0, 1, 2):
            prepare(c, 2)
            z_copy(c, 3).wait_recv()
            z_copy(c, 4).wait_recv()
            zr[c, 0] = zr[c, 0] + zr[c, 1] + own(c, 2)[...]
            go(z_copy(c, 2), early)
            prepare(c, -2)
            z_copy(c, -3).wait_recv()
            zr[c, 4] = zr[c, 4] + own(c, -2)[...]
            go(z_copy(c, -2), early)
        for c in (0, 1, 2):
            prepare(c, 1)
            z_copy(c, 2).wait_recv()
            zr[c, 2] = zr[c, 2] + own(c, 1)[...]
            go(z_copy(c, 1), early)
            prepare(c, -1)
            z_copy(c, -2).wait_recv()
            zr[c, 5] = zr[c, 5] + own(c, -1)[...]
            go(z_copy(c, -1), early)
        prepare(2, 0)

        def last(c):
            z_copy(c, 1).wait_recv()
            z_copy(c, -1).wait_recv()
            return own(c, 0)[...] + zr[c, 3] + zr[c, 6]

        xa[0] = last(0)
        x_last = remote(xa.at[0], xa.at[1], x_s.at[nz], x_r.at[nz], across)
        go(x_last, late)
        mine = last(1)
        sum_b = last(2)
        hs[0] = sum_b[0:2]
        hs[1] = sum_b[6:8]
        h_up = remote(hs.at[1], hr.at[0], h_s.at[1], h_r.at[0], above)
        h_down = remote(hs.at[0], hr.at[1], h_s.at[0], h_r.at[1], below)
        go(h_up, late)
        go(h_down, late)

        width = field.shape[1]
        col = iota((32, width), 1)

        def wrapped(values):
            right = pltpu.roll(values, lon, 1)
            left = pltpu.roll(values, width - lon, 1)
            return jnp.where(col < lon, values, jnp.where(col < (lon + width) // 2, right, left))

        @pl.when(it == 0)
        def _():
            for copy in d_copies:
                copy.wait_recv()
            dcoef[6:8, :lon] = dr[0]
            dcoef[24:26, :lon] = dr[1]
            dcoef[...] = wrapped(dcoef[...])

        field[8:12, :lon] = sum_b[0:4]
        field[20:24, :lon] = sum_b[4:8]
        for copy in early:
            copy.wait_send()
        x_last.wait_recv()
        field[12:20, :lon] = mine + xa[1]
        h_up.wait_recv()
        h_down.wait_recv()
        field[6:8, :lon] = hr[0]
        field[24:26, :lon] = hr[1]
        local_row = iota((32, width), 0) - 8
        global_row = local_row + tile * lat_rows
        inside = (global_row >= 0) & (global_row < lat_total) & (local_row >= -2) & (local_row < 18)
        f = jnp.where(inside, wrapped(field[...]), 0.0)
        north = ncoef[:, 0:1]
        south = scoef[:, 0:1]
        for _pass in range(2):
            east = pltpu.roll(f, width - 1, 1)
            west = pltpu.roll(f, 1, 1)
            upper = pltpu.roll(f, 31, 0)
            lower = pltpu.roll(f, 1, 0)
            change = SHRINK * (east + west - 2.0 * f) + north * (upper - f) + south * (lower - f)
            f = jnp.where(inside, f + dcoef[...] * change, 0.0)
        smoothed = f[8:24, :lon]
        shrunk = jnp.maximum(jnp.abs(smoothed) - thr_ref[tm], 0.0)
        pruned = jnp.where(smoothed < 0.0, -shrunk, shrunk)
        ga[z, u] = pruned[4:12]
        gb[z, u] = jnp.concatenate([pruned[0:4], pruned[12:16]], axis=0)

        def g_ref(c, off):
            if c == 0:
                return ga.at[zat(off), u]
            if c == 1:
                return gb.at[zat(off), u]
            return ga.at[zat(off), v]

        def g_copy(c, off):
            from_here = {1: 0, 2: 0, 3: -2, 4: -3, -1: 0, -2: 1, -3: 2}[off]
            ref = g_ref(c, from_here)
            where = plus2 if off == 2 else plus if off > 0 else minus
            return remote(ref, ref, g_s.at[c, slots_g[off]], g_r.at[c, slots_g[off]], where)

        def g_wait(c, off):
            ref = g_ref(c, -off)
            remote(ref, ref, g_s.at[c, slots_g[off]], g_r.at[c, slots_g[off]], plus).wait_recv()

        slots_g = {1: 0, 2: 1, 3: 2, 4: 3, -1: 4, -2: 5, -3: 6}
        queue = []

        def y_send(off):
            ref = gb.at[zat(off), u]
            q = len(queue)
            queue.append(off)
            go(remote(ref, ref, y_s.at[q], y_r.at[q], across), late)

        a_mine = ga.at[z, u]
        go(remote(a_mine, a_mine, y_s.at[nz], y_r.at[nz], across), late)
        for c in (0, 1):
            for off in (2, -1, 1):
                go(g_copy(c, off), late)
        y_send(0)
        squares = jnp.sum(jnp.sum(pruned * pruned, axis=1, keepdims=True), axis=0, keepdims=True)
        tile_first(ITERS + it, jnp.broadcast_to(squares, (8, 128)))
        tile_second(ITERS + it)
        a_other = ga.at[z, v]
        remote(a_other, a_other, y_s.at[nz], y_r.at[nz], across).wait_recv()
        for off in (2, -1, 1):
            go(g_copy(2, off), late)
        for c in (0, 1, 2):
            g_wait(c, 2)
            go(g_copy(c, 3), late)
            g_wait(c, -1)
            go(g_copy(c, -2), late)
            g_wait(c, 1)
            if c == 1:
                for off in (-2, 1, -1):
                    y_send(off)
        here = tile_total(ITERS + it)
        fr[it, tm] = lax.rsqrt(here / cells + EPS)
        for j, (_, where) in enumerate(factor_to):
            go(remote(fr.at[it, tm], fr.at[it, tm], f_s.at[it, j], f_r.at[it, j], where), late)
        for c in (0, 1, 2):
            g_wait(c, 3)
            go(g_copy(c, 4), late)
            g_wait(c, -2)
            go(g_copy(c, -3), late)
            if c == 1:
                for off in (-3, 2):
                    y_send(off)
        for c in (1, 0, 2):
            g_wait(c, 4)
            g_wait(c, -3)
            if c == 1:
                for off in (-4, 3):
                    y_send(off)
        for j, (slot, where) in enumerate(factor_to):
            remote(fr.at[it, slot], fr.at[it, slot], f_s.at[it, j], f_r.at[it, j], where).wait_recv()
        every = fr[it][:, 0, :]
        every = jnp.where(lax.rem(iota((modes, 128), 1), 16) == iota((modes, 128), 0), every, 0.0)
        fac[...] = jnp.broadcast_to(jnp.sum(every, axis=0, keepdims=True), (8, 128))
        for q, off in enumerate(queue):
            ref = gb.at[zat(off), v]
            remote(ref, ref, y_s.at[q], y_r.at[q], across).wait_recv()

        @pl.when(it + 1 < ITERS)
        def _():
            msg[...] = partial_scores()

        for copy in late:
            copy.wait_send()
        return 0

    lax.fori_loop(0, ITERS, step, 0)

    picked = jnp.where(lane == mode_of, jnp.broadcast_to(fac[0:1], (rows, 128)), 0.0)
    column_factor = jnp.sum(picked, axis=1, keepdims=True)
    out_a = ga[...].reshape(rows, lon) * column_factor
    out_b = gb[...].reshape(rows, lon) * column_factor
    for m in range(modes):
        c = (m % nz) * 16 + (m // nz) * 8
        cur_out[m, 4:12] = out_a[c : c + 8]
        cur_out[m, 0:4] = out_b[c : c + 4]
        cur_out[m, 12:16] = out_b[c + 4 : c + 8]
    for b in range(4):
        moved = sval[...] if b == 0 else pltpu.roll(sval[...], 128 - 16 * b, 1)
        sc_out[b * 8 : (b + 1) * 8, :] = moved[:, :16]
    for copy in d_copies:
        copy.wait_send()


def solution(mesh):
    nz = mesh.shape["tm"] // 2
    ny = mesh.shape["tile"] // 4

    def local(anomalies, initial, diffusivity, land_mask, threshold):
        times, lat_rows, lon = anomalies.shape
        modes = initial.shape[0]
        lat_total = lat_rows * mesh.shape["tile"]
        width = (lon + 127) // 128 * 128
        vmem = pltpu.VMEM
        dma = pltpu.SemaphoreType.DMA
        in_hbm = pl.BlockSpec(memory_space=pltpu.HBM)
        in_vmem = pl.BlockSpec(memory_space=pltpu.VMEM)
        half = (nz, 2, 8, lon)
        return pl.pallas_call(
            functools.partial(kernel, (nz, ny, lat_rows, lon, lat_total)),
            out_shape=(
                jax.ShapeDtypeStruct((modes, lat_rows, lon), F32),
                jax.ShapeDtypeStruct((times, modes), F32),
            ),
            in_specs=[in_hbm] * 5,
            out_specs=(in_vmem, in_vmem),
            scratch_shapes=[
                vmem((times * lat_rows, lon), BF16),
                vmem((modes, lat_rows, lon), BF16),
                vmem((lat_rows, lon), F32),
                vmem((lat_rows, lon), jnp.int32),
                pltpu.SMEM((modes,), F32),
                vmem(half, F32),
                vmem(half, F32),
                vmem(half, F32),
                vmem(half, F32),
                vmem((nz, 8, lon), F32),
                vmem((2, 8, lon), F32),
                vmem((3, nz - 1, 8, lon), F32),
                vmem((2 * ITERS, 2, 8, 128), F32),
                vmem((2 * ITERS, 2 * ny, 8, 128), F32),
                vmem((ITERS, modes, 8, 128), F32),
                vmem((2, 2, lon), F32),
                vmem((2, 2, lon), F32),
                vmem((2, 2, lon), F32),
                vmem((2, 2, lon), F32),
                vmem((32, width), F32),
                vmem((32, width), F32),
                vmem((32, 128), F32),
                vmem((32, 128), F32),
                vmem((8, 128), F32),
                vmem((8, 128), F32),
                vmem((8, 128), F32),
                dma((5,)),
                dma((3, nz - 1)),
                dma((3, nz - 1)),
                dma((nz + 1,)),
                dma((nz + 1,)),
                dma((3, nz - 1)),
                dma((3, nz - 1)),
                dma((nz + 1,)),
                dma((nz + 1,)),
                dma((2 * ITERS,)),
                dma((2 * ITERS,)),
                dma((2 * ITERS, 2 * ny - 1)),
                dma((2 * ITERS, 2 * ny - 1)),
                dma((ITERS, modes - 1)),
                dma((ITERS, modes - 1)),
                dma((2,)),
                dma((2,)),
                dma((2,)),
                dma((2,)),
            ],
            compiler_params=pltpu.CompilerParams(
                collective_id=0, has_side_effects=True, vmem_limit_bytes=60 * 1024 * 1024
            ),
        )(anomalies.reshape(times * lat_rows, lon), initial, diffusivity, land_mask, threshold)

    return jax.shard_map(
        local,
        mesh=mesh,
        in_specs=(
            P("tm", "tile", None),
            P(None, "tile", None),
            P("tile", None),
            P("tile", None),
            P(),
        ),
        out_specs=(P(None, "tile", None), P("tm", None)),
        check_vma=False,
    )
```

time: 132 us -> 119 us (0.902)
  Pallas kernels: 124 us -> 114 us
  local copies, waits for them, and re-layouts: 6.78 us -> 4.08 us
    pallas_call x1, Pallas kernels: 124 us -> 114 us  [local(): pl.pallas_call(functools.partial(kernel, (nz, ny, lat_rows, lon, lat_tota...]
    unnamed x11 -> x1, local copies, waits for them, and re-layouts: 6.11 us -> 2.69 us
where the time goes in v2:
time: 119 us
  Pallas kernels  114 us (96%)
  local copies, waits for them, and re-layouts  4.08 us (3%)
    pallas_call x1, Pallas kernels, local(): pl.pallas_call(functools.partial(kernel, (nz, ny, lat_rows, lon, lat_tota...  114 us
    unnamed x1, local copies, waits for them, and re-layouts  2.69 us

profile of v2, /device:TPU:1, one launch (start us, length us, event | category | flops | bytes accessed | tf_op | source)
XLA Modules:
  0.0 118.8 jit_solution(13692814706588266790)
XLA Ops:
  0.6 114.1 %shard_map.68 = (f32[16,16,1440]{2,1,0:T(8,128)}, f32[32,16]{1,0:T(8,128)}) custom-call(bf16[512,1440]{1,0:T(8,128)(2,1)} %bitcast.1, bf16[16,16,1440]{2,1,0:T(8,128)(2,1)} %init_hbm.1, f32[16,1440]{1,0:T(8,128)} %diff_hbm.1, s32[16,1440]{1,0:T(8,128)} %land_hbm.1, f32[16]{0:T(128)} %thr_hbm.1), custom_call_target="tpu_custom_call" | custom-call | tf_op jit(solution)/shard_map/pallas_call | solution.py:497
  114.7 1.4 %copy.7 = f32[32,16]{0,1:T(8,128)} copy(f32[32,16]{1,0:T(8,128)} %get-tuple-element.3) | data formatting | bytes 4096 | tf_op jit(solution)/shard_map/pallas_call | solution.py:497
  116.1 2.7 %copy.9 = f32[16,16,1440]{2,1,0:T(8,128)} copy(f32[16,16,1440]{2,1,0:T(8,128)} %get-tuple-element.6) | data formatting | bytes 2949120

commit v3 on v2

--- a/solution.py
+++ b/solution.py
@@ -27,8 +27,10 @@
     diff_hbm,
     land_hbm,
     thr_hbm,
-    cur_out,
-    sc_out,
+    ga_out,
+    gb_out,
+    fac_out,
+    score_out,
     anom,
     init,
     diff,
@@ -94,8 +96,10 @@
     plus = {"tm": u * nz + zat(1)}
     plus2 = {"tm": u * nz + zat(2)}
     minus = {"tm": u * nz + zat(-1)}
-    minus2 = {"tm": u * nz + zat(-2)}
     across = {"tm": v * nz + z}
+    plus_across = {"tm": v * nz + zat(1)}
+    plus2_across = {"tm": v * nz + zat(2)}
+    minus_across = {"tm": v * nz + zat(-1)}
     below = {"tile": lax.rem(tile + ntile - 1, ntile)}
     above = {"tile": lax.rem(tile + 1, ntile)}
     mate = {"tile": tile + sg}
@@ -143,27 +147,14 @@
     mode_of = lax.rem(lax.div(c_col, 8), 2) * nz + lax.div(c_col, 16)
 
     def row_in_band(i):
-        return i + 4, jnp.where(i < 4, i, i + 8)
-
-    loads[2].wait()
-    loads[3].wait()
-    dcoef[...] = jnp.zeros_like(dcoef)
-    diffuse = diff[...] * (1.0 + land[...].astype(F32)) * 0.5
-    dcoef[8:24, :lon] = diffuse
-    ds[0] = diffuse[0:2]
-    ds[1] = diffuse[14:16]
-    row_index = (tile * lat_rows + iota((32, 128), 0) - 8).astype(F32)
-    centre = jnp.sin(jnp.pi * (row_index + 0.5) / lat_total)
-    ncoef[...] = SHRINK * jnp.sin(jnp.pi * (row_index + 1.0) / lat_total) / centre
-    scoef[...] = SHRINK * jnp.sin(jnp.pi * row_index / lat_total) / centre
+        return jnp.where(i < 4, i, i + 8), i + 4
 
     loads[0].wait()
     for m in range(modes):
         wide = init[m].astype(F32)
-        ga[m % nz, m // nz] = wide[4:12]
-        gb[m % nz, m // nz] = jnp.concatenate([wide[0:4], wide[12:16]], axis=0)
+        ga[m % nz, m // nz] = jnp.concatenate([wide[0:4], wide[12:16]], axis=0)
+        gb[m % nz, m // nz] = wide[4:12]
     loads[1].wait()
-    loads[4].wait()
 
     def square_row():
         a = ga[...].reshape(rows, lon)
@@ -203,8 +194,22 @@
         remote(ds.at[0], dr.at[1], d_s.at[0], d_r.at[1], below),
         remote(ds.at[1], dr.at[0], d_s.at[1], d_r.at[0], above),
     ]
-    for copy in d_copies:
-        copy.start()
+
+    def coefficients():
+        loads[2].wait()
+        loads[3].wait()
+        dcoef[...] = jnp.zeros_like(dcoef)
+        diffuse = diff[...] * (1.0 + land[...].astype(F32)) * 0.5
+        dcoef[8:24, :lon] = diffuse
+        ds[0] = diffuse[0:2]
+        ds[1] = diffuse[14:16]
+        row_index = (tile * lat_rows + iota((32, 128), 0) - 8).astype(F32)
+        centre = jnp.sin(jnp.pi * (row_index + 0.5) / lat_total)
+        ncoef[...] = SHRINK * jnp.sin(jnp.pi * (row_index + 1.0) / lat_total) / centre
+        scoef[...] = SHRINK * jnp.sin(jnp.pi * row_index / lat_total) / centre
+        for copy in d_copies:
+            copy.start()
+        loads[4].wait()
 
     def step(it, _):
         late = []
@@ -232,6 +237,7 @@
 
         tile_first(it, msg[...])
         tile_second(it)
+        pl.when(it == 0)(coefficients)
         total = tile_total(it)
 
         @pl.when(it == 0)
@@ -284,14 +290,17 @@
             else:
                 src = zr.at[c, {2: 0, 1: 2, -2: 4, -1: 5}[off]]
             where = plus2 if off == 4 else plus if off > 0 else minus
+            if c == 0 and off in (1, -1):
+                where = plus_across if off > 0 else minus_across
             return remote(src, zr.at[c, slot], z_s.at[c, slot], z_r.at[c, slot], where)
 
         for copy in x_in[:3]:
             go(copy, late)
+        x_own = remote(pa.at[z, v], xa, x_s.at[nz], x_r.at[nz], across)
         for c in (0, 1):
             for off in (4, 3, -3):
                 go(z_copy(c, off), early)
-        for copy in x_in[3:]:
+        for copy in x_in[3:] + [x_own]:
             go(copy, late)
         for off in (4, 3, -3):
             prepare(2, off)
@@ -315,24 +324,21 @@
             z_copy(c, -2).wait_recv()
             zr[c, 5] = zr[c, 5] + own(c, -1)[...]
             go(z_copy(c, -1), early)
-        prepare(2, 0)
-
         def last(c):
             z_copy(c, 1).wait_recv()
             z_copy(c, -1).wait_recv()
-            return own(c, 0)[...] + zr[c, 3] + zr[c, 6]
-
-        xa[0] = last(0)
-        x_last = remote(xa.at[0], xa.at[1], x_s.at[nz], x_r.at[nz], across)
-        go(x_last, late)
-        mine = last(1)
-        sum_b = last(2)
-        hs[0] = sum_b[0:2]
-        hs[1] = sum_b[6:8]
+            return zr[c, 3] + zr[c, 6]
+
+        x_own.wait_recv()
+        sum_a = (pa[z, u] + xa[...]) + last(0) + last(1)
+        hs[0] = sum_a[0:2]
+        hs[1] = sum_a[6:8]
         h_up = remote(hs.at[1], hr.at[0], h_s.at[1], h_r.at[0], above)
         h_down = remote(hs.at[0], hr.at[1], h_s.at[0], h_r.at[1], below)
         go(h_up, late)
         go(h_down, late)
+        prepare(2, 0)
+        sum_b = xb[place[0]] + last(2)
 
         width = field.shape[1]
         col = iota((32, width), 1)
@@ -350,12 +356,11 @@
             dcoef[24:26, :lon] = dr[1]
             dcoef[...] = wrapped(dcoef[...])
 
-        field[8:12, :lon] = sum_b[0:4]
-        field[20:24, :lon] = sum_b[4:8]
+        field[8:12, :lon] = sum_a[0:4]
+        field[20:24, :lon] = sum_a[4:8]
+        field[12:20, :lon] = sum_b
         for copy in early:
             copy.wait_send()
-        x_last.wait_recv()
-        field[12:20, :lon] = mine + xa[1]
         h_up.wait_recv()
         h_down.wait_recv()
         field[6:8, :lon] = hr[0]
@@ -376,8 +381,8 @@
         smoothed = f[8:24, :lon]
         shrunk = jnp.maximum(jnp.abs(smoothed) - thr_ref[tm], 0.0)
         pruned = jnp.where(smoothed < 0.0, -shrunk, shrunk)
-        ga[z, u] = pruned[4:12]
-        gb[z, u] = jnp.concatenate([pruned[0:4], pruned[12:16]], axis=0)
+        ga[z, u] = jnp.concatenate([pruned[0:4], pruned[12:16]], axis=0)
+        gb[z, u] = pruned[4:12]
 
         def g_ref(c, off):
             if c == 0:
@@ -390,6 +395,9 @@
             from_here = {1: 0, 2: 0, 3: -2, 4: -3, -1: 0, -2: 1, -3: 2}[off]
             ref = g_ref(c, from_here)
             where = plus2 if off == 2 else plus if off > 0 else minus
+            if c == 2 and off in (1, 2, -1):
+                ref = ga.at[z, u]
+                where = {1: plus_across, 2: plus2_across, -1: minus_across}[off]
             return remote(ref, ref, g_s.at[c, slots_g[off]], g_r.at[c, slots_g[off]], where)
 
         def g_wait(c, off):
@@ -399,26 +407,23 @@
         slots_g = {1: 0, 2: 1, 3: 2, 4: 3, -1: 4, -2: 5, -3: 6}
         queue = []
 
-        def y_send(off):
+        def y_send(off, ahead=0):
             ref = gb.at[zat(off), u]
             q = len(queue)
-            queue.append(off)
-            go(remote(ref, ref, y_s.at[q], y_r.at[q], across), late)
-
+            queue.append(off - ahead)
+            where = {0: across, 1: plus_across, -1: minus_across}[ahead]
+            go(remote(ref, ref, y_s.at[q], y_r.at[q], where), late)
+
+        for off in (2, -1, 1):
+            for c in (0, 2, 1):
+                go(g_copy(c, off), late)
         a_mine = ga.at[z, u]
         go(remote(a_mine, a_mine, y_s.at[nz], y_r.at[nz], across), late)
-        for c in (0, 1):
-            for off in (2, -1, 1):
-                go(g_copy(c, off), late)
         y_send(0)
         squares = jnp.sum(jnp.sum(pruned * pruned, axis=1, keepdims=True), axis=0, keepdims=True)
         tile_first(ITERS + it, jnp.broadcast_to(squares, (8, 128)))
         tile_second(ITERS + it)
-        a_other = ga.at[z, v]
-        remote(a_other, a_other, y_s.at[nz], y_r.at[nz], across).wait_recv()
-        for off in (2, -1, 1):
-            go(g_copy(2, off), late)
-        for c in (0, 1, 2):
+        for c in (1, 0, 2):
             g_wait(c, 2)
             go(g_copy(c, 3), late)
             g_wait(c, -1)
@@ -431,20 +436,22 @@
         fr[it, tm] = lax.rsqrt(here / cells + EPS)
         for j, (_, where) in enumerate(factor_to):
             go(remote(fr.at[it, tm], fr.at[it, tm], f_s.at[it, j], f_r.at[it, j], where), late)
-        for c in (0, 1, 2):
+        for c in (1, 0, 2):
             g_wait(c, 3)
             go(g_copy(c, 4), late)
+            if c == 1:
+                y_send(-3, 1)
             g_wait(c, -2)
             go(g_copy(c, -3), late)
             if c == 1:
-                for off in (-3, 2):
-                    y_send(off)
+                y_send(2, -1)
+                y_send(-3)
+                y_send(2)
+        a_other = ga.at[z, v]
+        remote(a_other, a_other, y_s.at[nz], y_r.at[nz], across).wait_recv()
         for c in (1, 0, 2):
             g_wait(c, 4)
             g_wait(c, -3)
-            if c == 1:
-                for off in (-4, 3):
-                    y_send(off)
         for j, (slot, where) in enumerate(factor_to):
             remote(fr.at[it, slot], fr.at[it, slot], f_s.at[it, j], f_r.at[it, j], where).wait_recv()
         every = fr[it][:, 0, :]
@@ -464,20 +471,33 @@
 
     lax.fori_loop(0, ITERS, step, 0)
 
-    picked = jnp.where(lane == mode_of, jnp.broadcast_to(fac[0:1], (rows, 128)), 0.0)
-    column_factor = jnp.sum(picked, axis=1, keepdims=True)
-    out_a = ga[...].reshape(rows, lon) * column_factor
-    out_b = gb[...].reshape(rows, lon) * column_factor
-    for m in range(modes):
-        c = (m % nz) * 16 + (m // nz) * 8
-        cur_out[m, 4:12] = out_a[c : c + 8]
-        cur_out[m, 0:4] = out_b[c : c + 4]
-        cur_out[m, 12:16] = out_b[c + 4 : c + 8]
-    for b in range(4):
-        moved = sval[...] if b == 0 else pltpu.roll(sval[...], 128 - 16 * b, 1)
-        sc_out[b * 8 : (b + 1) * 8, :] = moved[:, :16]
+    stores = [
+        pltpu.make_async_copy(ga, ga_out, load_sem.at[0]),
+        pltpu.make_async_copy(gb, gb_out, load_sem.at[1]),
+    ]
+    for copy in stores:
+        copy.start()
+    fac_out[...] = fac[...]
+    score_out[...] = sval[...]
     for copy in d_copies:
         copy.wait_send()
+    for copy in stores:
+        copy.wait()
+
+
+def finish(nz, ga, gb, fac, sval, cur_out, score_out):
+    at = pl.program_id(0) * 2
+    lane = iota((1, 128), 1)
+    for b in range(2):
+        for u in range(2):
+            factor = jnp.sum(jnp.where(lane == u * nz + at + b, fac[0:1], 0.0), axis=1, keepdims=True)
+            half_a = ga[b, u] * factor
+            cur_out[u, b, 0:4] = half_a[0:4]
+            cur_out[u, b, 4:12] = gb[b, u] * factor
+            cur_out[u, b, 12:16] = half_a[4:8]
+    turned = sval[...].T
+    for b in range(4):
+        score_out[:, b * 8 : (b + 1) * 8] = turned[b * 16 : (b + 1) * 16]
 
 
 def solution(mesh):
@@ -494,14 +514,16 @@
         in_hbm = pl.BlockSpec(memory_space=pltpu.HBM)
         in_vmem = pl.BlockSpec(memory_space=pltpu.VMEM)
         half = (nz, 2, 8, lon)
-        return pl.pallas_call(
+        ga, gb, fac, sval = pl.pallas_call(
             functools.partial(kernel, (nz, ny, lat_rows, lon, lat_total)),
             out_shape=(
-                jax.ShapeDtypeStruct((modes, lat_rows, lon), F32),
-                jax.ShapeDtypeStruct((times, modes), F32),
+                jax.ShapeDtypeStruct(half, F32),
+                jax.ShapeDtypeStruct(half, F32),
+                jax.ShapeDtypeStruct((8, 128), F32),
+                jax.ShapeDtypeStruct((8, 128), F32),
             ),
             in_specs=[in_hbm] * 5,
-            out_specs=(in_vmem, in_vmem),
+            out_specs=(in_hbm, in_hbm, in_vmem, in_vmem),
             scratch_shapes=[
                 vmem((times * lat_rows, lon), BF16),
                 vmem((modes, lat_rows, lon), BF16),
@@ -513,7 +535,7 @@
                 vmem(half, F32),
                 vmem(half, F32),
                 vmem((nz, 8, lon), F32),
-                vmem((2, 8, lon), F32),
+                vmem((8, lon), F32),
                 vmem((3, nz - 1, 8, lon), F32),
                 vmem((2 * ITERS, 2, 8, 128), F32),
                 vmem((2 * ITERS, 2 * ny, 8, 128), F32),
@@ -553,6 +575,22 @@
                 collective_id=0, has_side_effects=True, vmem_limit_bytes=60 * 1024 * 1024
             ),
         )(anomalies.reshape(times * lat_rows, lon), initial, diffusivity, land_mask, threshold)
+        small = pl.BlockSpec((8, 128), lambda i: (0, 0))
+        block = pl.BlockSpec((2, 2, 8, lon), lambda i: (i, 0, 0, 0))
+        current, scores = pl.pallas_call(
+            functools.partial(finish, nz),
+            grid=(nz // 2,),
+            out_shape=(
+                jax.ShapeDtypeStruct((2, nz, lat_rows, lon), F32),
+                jax.ShapeDtypeStruct((modes, times), F32),
+            ),
+            in_specs=[block, block, small, small],
+            out_specs=(
+                pl.BlockSpec((2, 2, lat_rows, lon), lambda i: (0, i, 0, 0)),
+                pl.BlockSpec((modes, times), lambda i: (0, 0)),
+            ),
+        )(ga, gb, fac, sval)
+        return current.reshape(modes, lat_rows, lon), scores.T
 
     return jax.shard_map(
         local,

time: 119 us -> 115 us (0.966)
  local copies, waits for them, and re-layouts: 4.08 us -> 0 us
    pallas_call x0 -> x1, Pallas kernels: none -> 3.9 us  [local(): pl.pallas_call(functools.partial(finish, nz), grid=(nz // 2,), out_shape=...]
    pallas_call x1, Pallas kernels: 114 us -> 110 us  [local(): pl.pallas_call(functools.partial(kernel, (nz, ny, lat_rows, lon, lat_tota...]
    unnamed x1 -> x0, local copies, waits for them, and re-layouts: 2.69 us -> none
    pallas_call x1 -> x0, local copies, waits for them, and re-layouts: 1.39 us -> none  [local(): pl.pallas_call(functools.partial(kernel, (nz, ny, lat_rows, lon, lat_tota...]
where the time goes in v3:
time: 115 us
  Pallas kernels  114 us (99%)
    pallas_call x1, Pallas kernels, local(): pl.pallas_call(functools.partial(kernel, (nz, ny, lat_rows, lon, lat_tota...  110 us
    pallas_call x1, Pallas kernels, local(): pl.pallas_call(functools.partial(finish, nz), grid=(nz // 2,), out_shape=...  3.9 us

profile of v3, /device:TPU:1, one launch (start us, length us, event | category | flops | bytes accessed | tf_op | source)
XLA Modules:
  0.0 114.7 jit_solution(13401061093699454235)
XLA Ops:
  0.6 110.2 %shard_map.68 = (f32[8,2,8,1440]{3,2,1,0:T(8,128)}, f32[8,2,8,1440]{3,2,1,0:T(8,128)}, f32[8,128]{1,0:T(8,128)}, f32[8,128]{1,0:T(8,128)}) custom-call(bf16[512,1440]{1,0:T(8,128)(2,1)} %bitcast.3, bf16[16,16,1440]{2,1,0:T(8,128)(2,1)} %init_hbm.1, f32[16,1440]{1,0:T(8,128)} %diff_hbm.1, s32[16,1440]{1,0:T(8,128)} %land_hbm.1, f32[16]{0:T(128)} %thr_hbm.1), custom_call_target="tpu_custom_call" | custom-call | tf_op jit(solution)/shard_map/pallas_call | solution.py:517
  110.8 3.9 %shard_map.69 = (f32[2,8,16,1440]{3,2,1,0:T(8,128)}, f32[16,32]{1,0:T(8,128)}) custom-call(f32[8,2,8,1440]{3,2,1,0:T(8,128)} %get-tuple-element.8.ga, f32[8,2,8,1440]{3,2,1,0:T(8,128)} %get-tuple-element.9.gb, f32[8,128]{1,0:T(8,128)} %get-tuple-element.10.fac, f32[8,128]{1,0:T(8,128)} %get-tuple-element.11.sval), custom_call_target="tpu_custom_call" | custom-call | tf_op jit(solution)/shard_map/pallas_call | solution.py:580

commit v4 on v3

--- a/solution.py
+++ b/solution.py
@@ -45,6 +45,8 @@
     zr,
     s1,
     s2,
+    q1,
+    q2,
     fr,
     hs,
     hr,
@@ -98,7 +100,6 @@
     minus = {"tm": u * nz + zat(-1)}
     across = {"tm": v * nz + z}
     plus_across = {"tm": v * nz + zat(1)}
-    plus2_across = {"tm": v * nz + zat(2)}
     minus_across = {"tm": v * nz + zat(-1)}
     below = {"tile": lax.rem(tile + ntile - 1, ntile)}
     above = {"tile": lax.rem(tile + 1, ntile)}
@@ -218,27 +219,27 @@
             copy.start()
             waits.append(copy)
 
-        def tile_first(at, message):
-            s1[at, core] = message
-            go(remote(s1.at[at, core], s1.at[at, core], a1_s.at[at], a1_r.at[at], mate), late)
-
-        def tile_second(at):
-            other = s1.at[at, 1 - core]
+        def tile_first(one, at, message):
+            one[it, core] = message
+            go(remote(one.at[it, core], one.at[it, core], a1_s.at[at], a1_r.at[at], mate), late)
+
+        def tile_second(one, two, at):
+            other = one.at[it, 1 - core]
             remote(other, other, a1_s.at[at], a1_r.at[at], mate).wait_recv()
             me = y * 2 + xh
-            s2[at, me] = s1[at, 0] + s1[at, 1]
+            two[it, me] = one[it, 0] + one[it, 1]
             for j, (_, where) in enumerate(spread_to):
-                go(remote(s2.at[at, me], s2.at[at, me], a2_s.at[at, j], a2_r.at[at, j], where), late)
-
-        def tile_total(at):
+                go(remote(two.at[it, me], two.at[it, me], a2_s.at[at, j], a2_r.at[at, j], where), late)
+
+        def tile_total(two, at):
             for j, (slot, where) in enumerate(spread_to):
-                remote(s2.at[at, slot], s2.at[at, slot], a2_s.at[at, j], a2_r.at[at, j], where).wait_recv()
-            return jnp.sum(s2[at], axis=0)
-
-        tile_first(it, msg[...])
-        tile_second(it)
+                remote(two.at[it, slot], two.at[it, slot], a2_s.at[at, j], a2_r.at[at, j], where).wait_recv()
+            return jnp.sum(two[it], axis=0)
+
+        tile_first(s1, it, msg[...])
+        tile_second(s1, s2, it)
         pl.when(it == 0)(coefficients)
-        total = tile_total(it)
+        total = tile_total(s2, it)
 
         @pl.when(it == 0)
         def _():
@@ -250,19 +251,19 @@
 
         tall = jnp.broadcast_to(scores.reshape(8, 1, 128), (8, 16, 128)).reshape(128, 128)
         tall = tall.T.astype(BF16)
-        left = []
+        left_a = []
+        left_b = []
         for b in range(4):
             pick = jnp.where(lane == b * 16 + mode_of, 1.0, 0.0).astype(BF16)
             wide = jnp.dot(pick, tall, preferred_element_type=F32)
             in_a, in_b = row_in_band(lax.rem(c_col, 8))
             here = lax.rem(lane, 16)
-            left.append(
-                jnp.concatenate([jnp.where(here == in_a, wide, 0.0), jnp.where(here == in_b, wide, 0.0)], axis=0).astype(BF16)
-            )
-        spread = jnp.concatenate(left, axis=1)
-        part = jnp.dot(spread, anom[...], preferred_element_type=F32)
-        pb[...] = part[rows:].reshape(nz, 2, 8, lon)
-        pa[...] = part[:rows].reshape(nz, 2, 8, lon)
+            left_a.append(jnp.where(here == in_a, wide, 0.0).astype(BF16))
+            left_b.append(jnp.where(here == in_b, wide, 0.0).astype(BF16))
+
+        def loadings(left):
+            part = jnp.dot(jnp.concatenate(left, axis=1), anom[...], preferred_element_type=F32)
+            return part.reshape(nz, 2, 8, lon)
 
         early = []
         offsets = (4, 3, -3, 2, -2, 1, -1, 0)
@@ -285,45 +286,56 @@
 
         def z_copy(c, off):
             slot = slots[off]
-            if off in (4, 3, -3):
+            if off in (4, -3) or (c == 2 and off == 3):
                 src = own(c, off)
+            elif off == 2:
+                src = zr.at[c, 0 if c == 2 else 1]
             else:
-                src = zr.at[c, {2: 0, 1: 2, -2: 4, -1: 5}[off]]
-            where = plus2 if off == 4 else plus if off > 0 else minus
+                src = zr.at[c, {3: 0, 1: 2, -2: 4, -1: 5}[off]]
+            where = plus if off > 0 else minus
+            if c == 2 and off == 4:
+                where = plus2
             if c == 0 and off in (1, -1):
                 where = plus_across if off > 0 else minus_across
             return remote(src, zr.at[c, slot], z_s.at[c, slot], z_r.at[c, slot], where)
 
+        def onward(c, arrived, off):
+            prepare(c, off)
+            slot = slots[arrived]
+            z_copy(c, arrived).wait_recv()
+            zr[c, slot] = zr[c, slot] + own(c, off)[...]
+            go(z_copy(c, off), early)
+
+        pb[...] = loadings(left_b)
         for copy in x_in[:3]:
             go(copy, late)
+        pa[...] = loadings(left_a)
+        for off in (4, -3):
+            for c in (0, 1):
+                go(z_copy(c, off), early)
         x_own = remote(pa.at[z, v], xa, x_s.at[nz], x_r.at[nz], across)
-        for c in (0, 1):
-            for off in (4, 3, -3):
-                go(z_copy(c, off), early)
         for copy in x_in[3:] + [x_own]:
             go(copy, late)
+        for c in (0, 1):
+            onward(c, 4, 3)
+            onward(c, -3, -2)
         for off in (4, 3, -3):
             prepare(2, off)
             go(z_copy(2, off), early)
-        for c in (0, 1, 2):
-            prepare(c, 2)
-            z_copy(c, 3).wait_recv()
-            z_copy(c, 4).wait_recv()
-            zr[c, 0] = zr[c, 0] + zr[c, 1] + own(c, 2)[...]
-            go(z_copy(c, 2), early)
-            prepare(c, -2)
-            z_copy(c, -3).wait_recv()
-            zr[c, 4] = zr[c, 4] + own(c, -2)[...]
-            go(z_copy(c, -2), early)
-        for c in (0, 1, 2):
-            prepare(c, 1)
-            z_copy(c, 2).wait_recv()
-            zr[c, 2] = zr[c, 2] + own(c, 1)[...]
-            go(z_copy(c, 1), early)
-            prepare(c, -1)
-            z_copy(c, -2).wait_recv()
-            zr[c, 5] = zr[c, 5] + own(c, -1)[...]
-            go(z_copy(c, -1), early)
+        for c in (0, 1):
+            onward(c, 3, 2)
+            onward(c, -2, -1)
+        prepare(2, 2)
+        z_copy(2, 3).wait_recv()
+        z_copy(2, 4).wait_recv()
+        zr[2, 0] = zr[2, 0] + zr[2, 1] + own(2, 2)[...]
+        go(z_copy(2, 2), early)
+        onward(2, -3, -2)
+        for c in (0, 1):
+            onward(c, 2, 1)
+        onward(2, 2, 1)
+        onward(2, -2, -1)
+
         def last(c):
             z_copy(c, 1).wait_recv()
             z_copy(c, -1).wait_recv()
@@ -392,12 +404,15 @@
             return ga.at[zat(off), v]
 
         def g_copy(c, off):
-            from_here = {1: 0, 2: 0, 3: -2, 4: -3, -1: 0, -2: 1, -3: 2}[off]
+            from_here = {1: 0, 2: -1, 3: -2, 4: -3, -1: 0, -2: 1, -3: 2}[off]
+            where = plus if off > 0 else minus
+            if c == 1 and off == 2:
+                from_here = 0
+                where = plus2
             ref = g_ref(c, from_here)
-            where = plus2 if off == 2 else plus if off > 0 else minus
-            if c == 2 and off in (1, 2, -1):
+            if c == 2 and off in (1, -1):
                 ref = ga.at[z, u]
-                where = {1: plus_across, 2: plus2_across, -1: minus_across}[off]
+                where = plus_across if off > 0 else minus_across
             return remote(ref, ref, g_s.at[c, slots_g[off]], g_r.at[c, slots_g[off]], where)
 
         def g_wait(c, off):
@@ -407,51 +422,57 @@
         slots_g = {1: 0, 2: 1, 3: 2, 4: 3, -1: 4, -2: 5, -3: 6}
         queue = []
 
-        def y_send(off, ahead=0):
+        def y_send(off):
             ref = gb.at[zat(off), u]
             q = len(queue)
-            queue.append(off - ahead)
-            where = {0: across, 1: plus_across, -1: minus_across}[ahead]
-            go(remote(ref, ref, y_s.at[q], y_r.at[q], where), late)
+            queue.append(off)
+            go(remote(ref, ref, y_s.at[q], y_r.at[q], across), late)
+
+        def pass_on(c, arrived, off):
+            g_wait(c, arrived)
+            go(g_copy(c, off), late)
 
         for off in (2, -1, 1):
-            for c in (0, 2, 1):
+            go(g_copy(1, off), late)
+        for off in (1, -1):
+            for c in (0, 2):
                 go(g_copy(c, off), late)
+        y_send(0)
         a_mine = ga.at[z, u]
         go(remote(a_mine, a_mine, y_s.at[nz], y_r.at[nz], across), late)
-        y_send(0)
         squares = jnp.sum(jnp.sum(pruned * pruned, axis=1, keepdims=True), axis=0, keepdims=True)
-        tile_first(ITERS + it, jnp.broadcast_to(squares, (8, 128)))
-        tile_second(ITERS + it)
-        for c in (1, 0, 2):
-            g_wait(c, 2)
-            go(g_copy(c, 3), late)
-            g_wait(c, -1)
-            go(g_copy(c, -2), late)
-            g_wait(c, 1)
-            if c == 1:
-                for off in (-2, 1, -1):
-                    y_send(off)
-        here = tile_total(ITERS + it)
+        tile_first(q1, ITERS + it, jnp.broadcast_to(squares, (1, 128)))
+        tile_second(q1, q2, ITERS + it)
+        pass_on(1, 2, 3)
+        pass_on(1, -1, -2)
+        g_wait(1, 1)
+        for off in (-2, 1, -1):
+            y_send(off)
+        for c in (0, 2):
+            pass_on(c, 1, 2)
+            pass_on(c, -1, -2)
+        here = tile_total(q2, ITERS + it)
         fr[it, tm] = lax.rsqrt(here / cells + EPS)
         for j, (_, where) in enumerate(factor_to):
             go(remote(fr.at[it, tm], fr.at[it, tm], f_s.at[it, j], f_r.at[it, j], where), late)
-        for c in (1, 0, 2):
-            g_wait(c, 3)
-            go(g_copy(c, 4), late)
-            if c == 1:
-                y_send(-3, 1)
-            g_wait(c, -2)
-            go(g_copy(c, -3), late)
-            if c == 1:
-                y_send(2, -1)
-                y_send(-3)
-                y_send(2)
+        pass_on(1, 3, 4)
+        pass_on(1, -2, -3)
+        for off in (-3, 2):
+            y_send(off)
+        for c in (0, 2):
+            pass_on(c, 2, 3)
+            pass_on(c, -2, -3)
+        g_wait(1, 4)
+        g_wait(1, -3)
+        for off in (-4, 3):
+            y_send(off)
+        for c in (0, 2):
+            pass_on(c, 3, 4)
+            g_wait(c, -3)
+        for c in (0, 2):
+            g_wait(c, 4)
         a_other = ga.at[z, v]
         remote(a_other, a_other, y_s.at[nz], y_r.at[nz], across).wait_recv()
-        for c in (1, 0, 2):
-            g_wait(c, 4)
-            g_wait(c, -3)
         for j, (slot, where) in enumerate(factor_to):
             remote(fr.at[it, slot], fr.at[it, slot], f_s.at[it, j], f_r.at[it, j], where).wait_recv()
         every = fr[it][:, 0, :]
@@ -486,9 +507,10 @@
 
 
 def finish(nz, ga, gb, fac, sval, cur_out, score_out):
-    at = pl.program_id(0) * 2
+    each = ga.shape[0]
+    at = pl.program_id(0) * each
     lane = iota((1, 128), 1)
-    for b in range(2):
+    for b in range(each):
         for u in range(2):
             factor = jnp.sum(jnp.where(lane == u * nz + at + b, fac[0:1], 0.0), axis=1, keepdims=True)
             half_a = ga[b, u] * factor
@@ -537,9 +559,11 @@
                 vmem((nz, 8, lon), F32),
                 vmem((8, lon), F32),
                 vmem((3, nz - 1, 8, lon), F32),
-                vmem((2 * ITERS, 2, 8, 128), F32),
-                vmem((2 * ITERS, 2 * ny, 8, 128), F32),
-                vmem((ITERS, modes, 8, 128), F32),
+                vmem((ITERS, 2, 8, 128), F32),
+                vmem((ITERS, 2 * ny, 8, 128), F32),
+                vmem((ITERS, 2, 1, 128), F32),
+                vmem((ITERS, 2 * ny, 1, 128), F32),
+                vmem((ITERS, modes, 1, 128), F32),
                 vmem((2, 2, lon), F32),
                 vmem((2, 2, lon), F32),
                 vmem((2, 2, lon), F32),
@@ -576,17 +600,17 @@
             ),
         )(anomalies.reshape(times * lat_rows, lon), initial, diffusivity, land_mask, threshold)
         small = pl.BlockSpec((8, 128), lambda i: (0, 0))
-        block = pl.BlockSpec((2, 2, 8, lon), lambda i: (i, 0, 0, 0))
+        block = pl.BlockSpec((nz // 2, 2, 8, lon), lambda i: (i, 0, 0, 0))
         current, scores = pl.pallas_call(
             functools.partial(finish, nz),
-            grid=(nz // 2,),
+            grid=(2,),
             out_shape=(
                 jax.ShapeDtypeStruct((2, nz, lat_rows, lon), F32),
                 jax.ShapeDtypeStruct((modes, times), F32),
             ),
             in_specs=[block, block, small, small],
             out_specs=(
-                pl.BlockSpec((2, 2, lat_rows, lon), lambda i: (0, i, 0, 0)),
+                pl.BlockSpec((2, nz // 2, lat_rows, lon), lambda i: (0, i, 0, 0)),
                 pl.BlockSpec((modes, times), lambda i: (0, 0)),
             ),
         )(ga, gb, fac, sval)

time: 115 us -> 112 us (0.974); the launches traced: 115 us -> 110 us
  Pallas kernels: 114 us -> 110 us
    pallas_call x1, Pallas kernels: 110 us -> 107 us  [local(): pl.pallas_call(functools.partial(kernel, (nz, ny, lat_rows, lon, lat_tota...]
    pallas_call x1, Pallas kernels: 3.9 us -> 2.43 us  [local(): pl.pallas_call(functools.partial(finish, nz), grid=(2,), out_shape=(jax.S...]
where the time goes in v4:
time: 112 us; the launch traced here: 110 us
  Pallas kernels  110 us (98%)
    pallas_call x1, Pallas kernels, local(): pl.pallas_call(functools.partial(kernel, (nz, ny, lat_rows, lon, lat_tota...  107 us
    pallas_call x1, Pallas kernels, local(): pl.pallas_call(functools.partial(finish, nz), grid=(2,), out_shape=(jax.S...  2.43 us

profile of v4, /device:TPU:1, one launch (start us, length us, event | category | flops | bytes accessed | tf_op | source)
XLA Modules:
  0.0 110.2 jit_solution(9185185992692579375)
XLA Ops:
  0.6 107.1 %shard_map.68 = (f32[8,2,8,1440]{3,2,1,0:T(8,128)}, f32[8,2,8,1440]{3,2,1,0:T(8,128)}, f32[8,128]{1,0:T(8,128)}, f32[8,128]{1,0:T(8,128)}) custom-call(bf16[512,1440]{1,0:T(8,128)(2,1)} %bitcast.3, bf16[16,16,1440]{2,1,0:T(8,128)(2,1)} %init_hbm.1, f32[16,1440]{1,0:T(8,128)} %diff_hbm.1, s32[16,1440]{1,0:T(8,128)} %land_hbm.1, f32[16]{0:T(128)} %thr_hbm.1), custom_call_target="tpu_custom_call" | custom-call | tf_op jit(solution)/shard_map/pallas_call | solution.py:539
  107.7 2.4 %shard_map.69 = (f32[2,8,16,1440]{3,2,1,0:T(8,128)}, f32[16,32]{1,0:T(8,128)}) custom-call(f32[8,2,8,1440]{3,2,1,0:T(8,128)} %get-tuple-element.8.ga, f32[8,2,8,1440]{3,2,1,0:T(8,128)} %get-tuple-element.9.gb, f32[8,128]{1,0:T(8,128)} %get-tuple-element.10.fac, f32[8,128]{1,0:T(8,128)} %get-tuple-element.11.sval), custom_call_target="tpu_custom_call" | custom-call | tf_op jit(solution)/shard_map/pallas_call | solution.py:604

commit v5 on v4

--- a/solution.py
+++ b/solution.py
@@ -82,6 +82,8 @@
     nz, ny, lat_rows, lon, lat_total = geo
     cells = lat_total * lon
     ntile = ny * 4
+    middle = (lon + 255) // 256 * 128
+    pieces = (pl.ds(0, middle), pl.ds(middle, lon - middle))
     tm = lax.axis_index("tm")
     tile = lax.axis_index("tile")
     u = lax.div(tm, nz)
@@ -284,7 +286,7 @@
                 x_in[q].wait_recv()
                 xb[q] = xb[q] + pb[zat(off), u]
 
-        def z_copy(c, off):
+        def z_copy(c, off, p):
             slot = slots[off]
             if off in (4, -3) or (c == 2 and off == 3):
                 src = own(c, off)
@@ -297,14 +299,22 @@
                 where = plus2
             if c == 0 and off in (1, -1):
                 where = plus_across if off > 0 else minus_across
-            return remote(src, zr.at[c, slot], z_s.at[c, slot], z_r.at[c, slot], where)
+            src = src.at[:, pieces[p]]
+            return remote(src, zr.at[c, slot, :, pieces[p]], z_s.at[c, p, slot], z_r.at[c, p, slot], where)
+
+        def start(c, off):
+            prepare(c, off)
+            for p in (0, 1):
+                go(z_copy(c, off, p), early)
 
         def onward(c, arrived, off):
             prepare(c, off)
             slot = slots[arrived]
-            z_copy(c, arrived).wait_recv()
-            zr[c, slot] = zr[c, slot] + own(c, off)[...]
-            go(z_copy(c, off), early)
+            for p in (0, 1):
+                z_copy(c, arrived, p).wait_recv()
+                cols = pieces[p]
+                zr[c, slot, :, cols] = zr[c, slot, :, cols] + own(c, off)[:, cols]
+                go(z_copy(c, off, p), early)
 
         pb[...] = loadings(left_b)
         for copy in x_in[:3]:
@@ -312,7 +322,7 @@
         pa[...] = loadings(left_a)
         for off in (4, -3):
             for c in (0, 1):
-                go(z_copy(c, off), early)
+                start(c, off)
         x_own = remote(pa.at[z, v], xa, x_s.at[nz], x_r.at[nz], across)
         for copy in x_in[3:] + [x_own]:
             go(copy, late)
@@ -320,16 +330,17 @@
             onward(c, 4, 3)
             onward(c, -3, -2)
         for off in (4, 3, -3):
-            prepare(2, off)
-            go(z_copy(2, off), early)
+            start(2, off)
         for c in (0, 1):
             onward(c, 3, 2)
             onward(c, -2, -1)
         prepare(2, 2)
-        z_copy(2, 3).wait_recv()
-        z_copy(2, 4).wait_recv()
-        zr[2, 0] = zr[2, 0] + zr[2, 1] + own(2, 2)[...]
-        go(z_copy(2, 2), early)
+        for p in (0, 1):
+            cols = pieces[p]
+            z_copy(2, 3, p).wait_recv()
+            z_copy(2, 4, p).wait_recv()
+            zr[2, 0, :, cols] = zr[2, 0, :, cols] + zr[2, 1, :, cols] + own(2, 2)[:, cols]
+            go(z_copy(2, 2, p), early)
         onward(2, -3, -2)
         for c in (0, 1):
             onward(c, 2, 1)
@@ -337,8 +348,9 @@
         onward(2, -2, -1)
 
         def last(c):
-            z_copy(c, 1).wait_recv()
-            z_copy(c, -1).wait_recv()
+            for p in (0, 1):
+                z_copy(c, 1, p).wait_recv()
+                z_copy(c, -1, p).wait_recv()
             return zr[c, 3] + zr[c, 6]
 
         x_own.wait_recv()
@@ -403,7 +415,7 @@
                 return gb.at[zat(off), u]
             return ga.at[zat(off), v]
 
-        def g_copy(c, off):
+        def g_copy(c, off, p):
             from_here = {1: 0, 2: -1, 3: -2, 4: -3, -1: 0, -2: 1, -3: 2}[off]
             where = plus if off > 0 else minus
             if c == 1 and off == 2:
@@ -413,11 +425,20 @@
             if c == 2 and off in (1, -1):
                 ref = ga.at[z, u]
                 where = plus_across if off > 0 else minus_across
-            return remote(ref, ref, g_s.at[c, slots_g[off]], g_r.at[c, slots_g[off]], where)
+            ref = ref.at[:, pieces[p]]
+            return remote(ref, ref, g_s.at[c, p, slots_g[off]], g_r.at[c, p, slots_g[off]], where)
+
+        def g_arrive(c, off, p):
+            ref = g_ref(c, -off).at[:, pieces[p]]
+            remote(ref, ref, g_s.at[c, p, slots_g[off]], g_r.at[c, p, slots_g[off]], plus).wait_recv()
 
         def g_wait(c, off):
-            ref = g_ref(c, -off)
-            remote(ref, ref, g_s.at[c, slots_g[off]], g_r.at[c, slots_g[off]], plus).wait_recv()
+            for p in (0, 1):
+                g_arrive(c, off, p)
+
+        def g_start(c, off):
+            for p in (0, 1):
+                go(g_copy(c, off, p), late)
 
         slots_g = {1: 0, 2: 1, 3: 2, 4: 3, -1: 4, -2: 5, -3: 6}
         queue = []
@@ -429,14 +450,15 @@
             go(remote(ref, ref, y_s.at[q], y_r.at[q], across), late)
 
         def pass_on(c, arrived, off):
-            g_wait(c, arrived)
-            go(g_copy(c, off), late)
+            for p in (0, 1):
+                g_arrive(c, arrived, p)
+                go(g_copy(c, off, p), late)
 
         for off in (2, -1, 1):
-            go(g_copy(1, off), late)
+            g_start(1, off)
         for off in (1, -1):
             for c in (0, 2):
-                go(g_copy(c, off), late)
+                g_start(c, off)
         y_send(0)
         a_mine = ga.at[z, u]
         go(remote(a_mine, a_mine, y_s.at[nz], y_r.at[nz], across), late)
@@ -576,12 +598,12 @@
                 vmem((8, 128), F32),
                 vmem((8, 128), F32),
                 dma((5,)),
-                dma((3, nz - 1)),
-                dma((3, nz - 1)),
+                dma((3, 2, nz - 1)),
+                dma((3, 2, nz - 1)),
                 dma((nz + 1,)),
                 dma((nz + 1,)),
-                dma((3, nz - 1)),
-                dma((3, nz - 1)),
+                dma((3, 2, nz - 1)),
+                dma((3, 2, nz - 1)),
                 dma((nz + 1,)),
                 dma((nz + 1,)),
                 dma((2 * ITERS,)),

time: 112 us -> 110 us (0.982)
  Pallas kernels: 110 us -> 108 us
    pallas_call x1, Pallas kernels: 107 us -> 106 us  [local(): pl.pallas_call(functools.partial(kernel, (nz, ny, lat_rows, lon, lat_tota...]
where the time goes in v5:
time: 110 us; the launch traced here: 109 us
  Pallas kernels  108 us (98%)
    pallas_call x1, Pallas kernels, local(): pl.pallas_call(functools.partial(kernel, (nz, ny, lat_rows, lon, lat_tota...  106 us
    pallas_call x1, Pallas kernels, local(): pl.pallas_call(functools.partial(finish, nz), grid=(2,), out_shape=(jax.S...  2.43 us

profile of v5, /device:TPU:1, one launch (start us, length us, event | category | flops | bytes accessed | tf_op | source)
XLA Modules:
  0.0 109.0 jit_solution(9299805306379803563)
XLA Ops:
  0.6 105.9 %shard_map.68 = (f32[8,2,8,1440]{3,2,1,0:T(8,128)}, f32[8,2,8,1440]{3,2,1,0:T(8,128)}, f32[8,128]{1,0:T(8,128)}, f32[8,128]{1,0:T(8,128)}) custom-call(bf16[512,1440]{1,0:T(8,128)(2,1)} %bitcast.3, bf16[16,16,1440]{2,1,0:T(8,128)(2,1)} %init_hbm.1, f32[16,1440]{1,0:T(8,128)} %diff_hbm.1, s32[16,1440]{1,0:T(8,128)} %land_hbm.1, f32[16]{0:T(128)} %thr_hbm.1), custom_call_target="tpu_custom_call" | custom-call | tf_op jit(solution)/shard_map/pallas_call | solution.py:561
  106.5 2.4 %shard_map.69 = (f32[2,8,16,1440]{3,2,1,0:T(8,128)}, f32[16,32]{1,0:T(8,128)}) custom-call(f32[8,2,8,1440]{3,2,1,0:T(8,128)} %get-tuple-element.8.ga, f32[8,2,8,1440]{3,2,1,0:T(8,128)} %get-tuple-element.9.gb, f32[8,128]{1,0:T(8,128)} %get-tuple-element.10.fac, f32[8,128]{1,0:T(8,128)} %get-tuple-element.11.sval), custom_call_target="tpu_custom_call" | custom-call | tf_op jit(solution)/shard_map/pallas_call | solution.py:626

commit v6 on v5

--- a/solution.py
+++ b/solution.py
@@ -473,10 +473,6 @@
         for c in (0, 2):
             pass_on(c, 1, 2)
             pass_on(c, -1, -2)
-        here = tile_total(q2, ITERS + it)
-        fr[it, tm] = lax.rsqrt(here / cells + EPS)
-        for j, (_, where) in enumerate(factor_to):
-            go(remote(fr.at[it, tm], fr.at[it, tm], f_s.at[it, j], f_r.at[it, j], where), late)
         pass_on(1, 3, 4)
         pass_on(1, -2, -3)
         for off in (-3, 2):
@@ -484,6 +480,10 @@
         for c in (0, 2):
             pass_on(c, 2, 3)
             pass_on(c, -2, -3)
+        here = tile_total(q2, ITERS + it)
+        fr[it, tm] = lax.rsqrt(here / cells + EPS)
+        for j, (_, where) in enumerate(factor_to):
+            go(remote(fr.at[it, tm], fr.at[it, tm], f_s.at[it, j], f_r.at[it, j], where), late)
         g_wait(1, 4)
         g_wait(1, -3)
         for off in (-4, 3):

time: 110 us -> 110 us (level)
  no operation moved by 1% of the time
where the time goes in v6:
time: 110 us
  Pallas kernels  109 us (99%)
    pallas_call x1, Pallas kernels, local(): pl.pallas_call(functools.partial(kernel, (nz, ny, lat_rows, lon, lat_tota...  107 us
    pallas_call x1, Pallas kernels, local(): pl.pallas_call(functools.partial(finish, nz), grid=(2,), out_shape=(jax.S...  2.43 us

profile of v6, /device:TPU:1, one launch (start us, length us, event | category | flops | bytes accessed | tf_op | source)
XLA Modules:
  0.0 109.8 jit_solution(8658829809113795903)
XLA Ops:
  0.6 106.7 %shard_map.68 = (f32[8,2,8,1440]{3,2,1,0:T(8,128)}, f32[8,2,8,1440]{3,2,1,0:T(8,128)}, f32[8,128]{1,0:T(8,128)}, f32[8,128]{1,0:T(8,128)}) custom-call(bf16[512,1440]{1,0:T(8,128)(2,1)} %bitcast.3, bf16[16,16,1440]{2,1,0:T(8,128)(2,1)} %init_hbm.1, f32[16,1440]{1,0:T(8,128)} %diff_hbm.1, s32[16,1440]{1,0:T(8,128)} %land_hbm.1, f32[16]{0:T(128)} %thr_hbm.1), custom_call_target="tpu_custom_call" | custom-call | tf_op jit(solution)/shard_map/pallas_call | solution.py:561
  107.3 2.4 %shard_map.69 = (f32[2,8,16,1440]{3,2,1,0:T(8,128)}, f32[16,32]{1,0:T(8,128)}) custom-call(f32[8,2,8,1440]{3,2,1,0:T(8,128)} %get-tuple-element.8.ga, f32[8,2,8,1440]{3,2,1,0:T(8,128)} %get-tuple-element.9.gb, f32[8,128]{1,0:T(8,128)} %get-tuple-element.10.fac, f32[8,128]{1,0:T(8,128)} %get-tuple-element.11.sval), custom_call_target="tpu_custom_call" | custom-call | tf_op jit(solution)/shard_map/pallas_call | solution.py:626
